TPU v7x, 128 devices: a whole 4x4x4 slice. The times are simulated.
128 devices in a mesh: gx: 16 (over z, y), gy: 8 (over x, core).
Axes of the slice: x: 4, y: 4, z: 4, core: 2. Of those that a mesh axis runs over, the one named last changes fastest.
Arguments:
- disp_now: float32 [3, 8, 256, 1024], P(None, None, 'gx', 'gy'), may hold values from -6 to 6
- disp_prev: float32 [3, 8, 256, 1024], P(None, None, 'gx', 'gy'), may hold values from -6 to 6
- density: float32 [8, 256, 1024], P(None, 'gx', 'gy'), may hold values from 1 to 2
- moduli: float32 [2, 8, 256, 1024], P(None, None, 'gx', 'gy'), may hold values from 0.3 to 1
- coarse: float32 [256, 24, 256], P(('gx', 'gy')), may hold values from -6 to 6
- block_route: int32 [256], replicated, may hold values from 0 to 511, as said below
- ranges: int32 [16, 8, 2], P('gx', 'gy'), may hold values from 1 to 8, as said below
- offsets: int32 [16, 8, 4, 3], P('gx', 'gy'), may hold values from 0 to 24, as said below
Outputs:
- incident: float32 [2, 3, 8, 256, 1024], P(None, None, None, 'gx', 'gy')
- disp_mid: float32 [3, 8, 256, 1024], P(None, None, 'gx', 'gy')
- disp_next: float32 [3, 8, 256, 1024], P(None, None, 'gx', 'gy')
Inputs may be any that keep to these rules, and one draw needn't show every extreme that they name: block_route[b] = tile 4 + g with tile = X 8 + Y; no slot is named twice; the slots named of a tile are g = 0 to k - 1 for its count k, which is 1 on half of the tiles, 2 on a quarter and 4 on a quarter. ranges[X, Y] = (lo, hi) with hi = 2 k for the tile's count k in block_route, and 1 <= lo < hi. offsets[X, Y, g] = (oz, oe, on) in fine cells with oz at most 5.
All inputs are finite; a program needn't handle non-finite values.
Results may differ from a plain program's by a relative error of at most 0.000073.
Values sent between devices are 32-bit elements; how exact they have to be, the bound alone decides.
A program may use at most 64 MiB of HBM per device.

v0:
```python
import jax
import jax.numpy as jnp
from jax import lax
from jax.sharding import PartitionSpec as P

step_square = 0.05
time_weights = ((-0.0595, 0.7735, 0.3315, -0.0455), (-0.063756, 0.607068, 0.517132, -0.060444))


def padded_2(cells, sides, width):
    for axis, dim in sides:
        count = lax.axis_size(axis)
        ends = count - 1
        head = lax.slice_in_dim(cells, 0, width, axis=dim)
        tail = lax.slice_in_dim(cells, cells.shape[dim] - width, cells.shape[dim], axis=dim)
        cells = jnp.concatenate(
            [
                lax.ppermute(tail, axis, [(i, (i + 1) % count) for i in range(ends)]),
                cells,
                lax.ppermute(head, axis, [((i + 1) % count, i) for i in range(ends)]),
            ],
            axis=dim,
        )
    return cells


def trimmed(values_in, axis_pos, head_cut, tail_cut):
    axis_pos = axis_pos % values_in.ndim
    return lax.slice_in_dim(
        values_in, head_cut, values_in.shape[axis_pos] - tail_cut, axis=axis_pos
    )


def inner_cut(values_in, axes_list):
    for axis_pos in axes_list:
        values_in = trimmed(values_in, axis_pos, 1, 1)
    return values_in


def operate(motion, shear_mod, lame_mod):
    spatial = (-3, -2, -1)
    stiffness = lame_mod + 2.0 * shear_mod
    components = []
    for i in range(3):
        component = motion[..., i, :, :, :]
        total = None
        for j in range(3):
            axis_along = spatial[j]
            others = tuple((a for a in spatial if a != axis_along))
            modulus = stiffness if j == i else shear_mod
            values = inner_cut(component, others)
            weights = inner_cut(modulus, others)
            middle = trimmed(values, axis_along, 1, 1)
            forward = trimmed(values, axis_along, 2, 0)
            backward = trimmed(values, axis_along, 0, 2)
            modulus_mid = trimmed(weights, axis_along, 1, 1)
            modulus_next = trimmed(weights, axis_along, 2, 0)
            modulus_prior = trimmed(weights, axis_along, 0, 2)
            flux_term = 0.5 * (modulus_mid + modulus_next) * (forward - middle) - 0.5 * (
                modulus_mid + modulus_prior
            ) * (middle - backward)
            total = flux_term if total is None else total + flux_term
        for j in range(3):
            if j != i:
                across = spatial[i]
                axis_along = spatial[j]
                third_axis = [a for a in spatial if a != across and a != axis_along][0]
                partner = motion[..., j, :, :, :]
                gradient = 0.5 * (
                    trimmed(partner, axis_along, 2, 0) - trimmed(partner, axis_along, 0, 2)
                )
                flux_term = trimmed(lame_mod, axis_along, 1, 1) * gradient
                total = total + trimmed(
                    0.5 * (trimmed(flux_term, across, 2, 0) - trimmed(flux_term, across, 0, 2)),
                    third_axis,
                    1,
                    1,
                )
                gradient = 0.5 * (trimmed(partner, across, 2, 0) - trimmed(partner, across, 0, 2))
                flux_term = trimmed(shear_mod, across, 1, 1) * gradient
                total = total + trimmed(
                    0.5
                    * (trimmed(flux_term, axis_along, 2, 0) - trimmed(flux_term, axis_along, 0, 2)),
                    third_axis,
                    1,
                    1,
                )
        components.append(total)
    return jnp.stack(components, axis=-4)


def hat_matrix(offset_cells, fine_count, coarse_count):
    fine_pos = (offset_cells[:, None] + jnp.arange(fine_count, dtype=jnp.int32)[None, :]) * 4
    base_index = fine_pos // 25
    fraction = (fine_pos % 25).astype(jnp.float32) / 25.0
    column = jnp.arange(coarse_count, dtype=jnp.int32)
    first = jnp.where(
        column[None, None, :] == base_index[:, :, None], 1.0 - fraction[:, :, None], 0.0
    )
    second = jnp.where(
        column[None, None, :] == base_index[:, :, None] + 1, fraction[:, :, None], 0.0
    )
    return first + second


def spread(samples, offset_cells, east_cells, north_cells):
    level_pos = (offset_cells[:, 0:1] + jnp.arange(2, dtype=jnp.int32)[None, :]).astype(
        jnp.float32
    ) * (4.0 / 25.0)
    upper_level = samples[:, :, :, 0][:, :, :, None]
    lower_level = samples[:, :, :, 1][:, :, :, None]
    vertical = (
        upper_level * (1.0 - level_pos)[:, None, None, :, None, None]
        + lower_level * level_pos[:, None, None, :, None, None]
    )
    east_matrix = hat_matrix(offset_cells[:, 1], east_cells, samples.shape[-2])
    north_matrix = hat_matrix(offset_cells[:, 2], north_cells, samples.shape[-1])
    eastern = jnp.einsum(
        "kxa,kncjay->kncjxy", east_matrix, vertical, precision=lax.Precision.HIGHEST
    )
    return jnp.einsum("kncjxa,kya->kncjxy", eastern, north_matrix, precision=lax.Precision.HIGHEST)


def level_pad(values_in):
    return jnp.pad(values_in, [(0, 0)] * (values_in.ndim - 3) + [(1, 1), (0, 0), (0, 0)])


def local(disp_now, disp_prev, density, moduli, coarse, block_route, ranges, offsets):
    levels = disp_now.shape[1]
    groups = levels // 2
    east_cells = disp_now.shape[2]
    north_cells = disp_now.shape[3]
    coarse_east = (east_cells + 23) * 4 // 25 + 2
    coarse_north = (north_cells + 23) * 4 // 25 + 2
    point_total = coarse_east * coarse_north
    block_hold = coarse.shape[0]
    samples_in = coarse.shape[1] // 6
    east_count = lax.axis_size("gx")
    north_count = lax.axis_size("gy")
    device_count = east_count * north_count
    own_east = lax.axis_index("gx")
    own_north = lax.axis_index("gy")
    own_flat = own_east * north_count + own_north
    start_pad = level_pad(
        padded_2(jnp.concatenate([moduli, disp_now], axis=0), (("gx", 2), ("gy", 3)), 1)
    )
    shear_mod = start_pad[0]
    lame_mod = start_pad[1]
    now_pad = start_pad[2:5]

    def advance(padded, current, previous, forcing):
        return (
            2.0 * current
            - previous
            + step_square / density * (operate(padded, shear_mod, lame_mod) + forcing)
        )

    weights = jnp.array(time_weights, jnp.float32)
    count_here = coarse.shape[0]
    width_here = coarse.shape[2]
    blended = jnp.einsum(
        "nt,ktpq->knpq",
        weights,
        coarse.reshape(count_here, samples_in, 6, width_here),
        precision=lax.Precision.HIGHEST,
    )
    payload = blended.reshape(count_here, 12, width_here)
    row_width = payload.shape[1]
    piece_width = payload.shape[2]
    group_ids = jnp.arange(groups, dtype=jnp.int32)
    local_tiles = lax.dynamic_slice_in_dim(block_route, own_flat * block_hold, block_hold) // groups
    targets = jnp.arange(device_count, dtype=jnp.int32)
    sending = (local_tiles[None, :] == targets[:, None]).astype(jnp.float32)
    outgoing = sending[:, :, None, None] * payload[None]
    received = lax.all_to_all(
        outgoing, ("gx", "gy"), split_axis=0, concat_axis=0, tiled=True
    ).reshape(device_count * block_hold, row_width, piece_width)
    select = (block_route[None, :] == own_flat * groups + group_ids[:, None]).astype(jnp.float32)
    arrived = jnp.einsum("gk,kpq->gpq", select, received, precision=lax.Precision.HIGHEST)
    slot_data = arrived[:, :, :point_total]
    samples = slot_data.reshape(groups, 2, 3, 2, coarse_east, coarse_north)
    fine_values = spread(samples, offsets[0, 0], east_cells, north_cells)
    incident = fine_values.transpose(1, 2, 0, 3, 4, 5).reshape(
        2, 3, levels, east_cells, north_cells
    )
    low_level = ranges[0, 0, 0]
    high_level = ranges[0, 0, 1]
    level_ids = jnp.arange(levels, dtype=jnp.int32)[:, None, None]
    outer_mask = (level_ids < low_level).astype(jnp.float32)
    inner_mask = ((level_ids >= low_level) & (level_ids < high_level)).astype(jnp.float32)
    masked = jnp.stack(
        [
            outer_mask * incident[0],
            inner_mask * incident[0],
            outer_mask * incident[1],
            inner_mask * incident[1],
        ]
    )
    padded_parts = level_pad(padded_2(masked, (("gx", 3), ("gy", 4)), 1))
    applied = operate(padded_parts, shear_mod, lame_mod)
    force_first = inner_mask * applied[0] - outer_mask * applied[1]
    force_second = inner_mask * applied[2] - outer_mask * applied[3]
    disp_mid = advance(now_pad, disp_now, disp_prev, force_first)
    mid_pad = level_pad(padded_2(disp_mid, (("gx", 2), ("gy", 3)), 1))
    disp_next = advance(mid_pad, disp_mid, disp_now, force_second)
    return (incident, disp_mid, disp_next)


def solution(mesh):
    return jax.shard_map(
        local,
        mesh=mesh,
        in_specs=(
            P(None, None, "gx", "gy"),
            P(None, None, "gx", "gy"),
            P(None, "gx", "gy"),
            P(None, None, "gx", "gy"),
            P(("gx", "gy"), None, None),
            P(),
            P("gx", "gy", None),
            P("gx", "gy", None, None),
        ),
        out_specs=(
            P(None, None, None, "gx", "gy"),
            P(None, None, "gx", "gy"),
            P(None, None, "gx", "gy"),
        ),
        check_vma=False,
    )
```

profile of v0, /device:TPU:27, one launch (start us, length us, event | category | flops | bytes accessed | tf_op | source)
XLA Modules:
  0.0 153.1 jit_solution(4829405271573514422)
XLA Ops:
  3.2 2.6 %broadcast_multiply_fusion = f32[128,2,12,256]{3,1,2,0:T(2,128)} fusion(f32[2,12,256]{2,0,1:T(2,128)S(1)} %bitcast.180, f32[128,2]{1,0:T(8,128)S(1)} %fusion.285), kind=kLoop, calls=%fused_computation.17 | loop fusion | flops 786432 | bytes 3171328 | tf_op jit(solution)/shard_map/mul | solution.py:174
  5.8 11.0 %all-to-all-start = ((f32[128,2,12,256]{3,1,2,0:T(2,128)}), f32[128,2,12,256]{3,1,2,0:T(2,128)}, u32[]{:S(2)}, u32[]{:S(2)}) async-start(f32[128,2,12,256]{3,1,2,0:T(2,128)} %broadcast_multiply_fusion), calls=%async_computation | async-start | bytes 6291456 | tf_op jit(solution)/shard_map/all_to_all | solution.py:175
  16.9 3.2 %collective-permute-start = (f32[5,8,1,128]{3,2,1,0:T(1,128)S(1)}, f32[5,8,1,128]{3,2,1,0:T(1,128)S(1)}, u32[]{:S(2)}, u32[]{:S(2)}) collective-permute-start(f32[5,8,1,128]{3,2,1,0:T(1,128)S(1)} %get-tuple-element.79), channel_id=1, source_target_pairs={{0,8},{8,16},{16,24},{24,32},{32,40},{40,48},{48,56},{56,64},{64,7... | collective-permute-start | bytes 61448 | tf_op jit(solution)/shard_map/ppermute | solution.py:18
  20.1 2.1 %collective-permute-start.1 = (f32[5,8,1,128]{3,2,1,0:T(1,128)S(1)}, f32[5,8,1,128]{3,2,1,0:T(1,128)S(1)}, u32[]{:S(2)}, u32[]{:S(2)}) collective-permute-start(f32[5,8,1,128]{3,2,1,0:T(1,128)S(1)} %get-tuple-element.80), channel_id=1, source_target_pairs={{8,0},{16,8},{24,16},{32,24},{40,32},{48,40},{56,48},{64,56},{72,6... | collective-permute-start | bytes 61448 | tf_op jit(solution)/shard_map/ppermute | solution.py:20
  24.2 1.3 compare_convert_fusion
  25.5 25.7 %collective-permute-done = f32[5,8,1,128]{3,2,1,0:T(1,128)S(1)} collective-permute-done((f32[5,8,1,128]{3,2,1,0:T(1,128)S(1)}, f32[5,8,1,128]{3,2,1,0:T(1,128)S(1)}, u32[]{:S(2)}, u32[]{:S(2)}) %collective-permute-start) | collective-permute-done | bytes 20512 | tf_op jit(solution)/shard_map/ppermute | solution.py:18
  51.5 3.8 %collective-permute-start.2 = (f32[5,8,18,1]{3,2,1,0:T(8,128)S(1)}, f32[5,8,18,1]{3,2,1,0:T(8,128)S(1)}, u32[]{:S(2)}, u32[]{:S(2)}) collective-permute-start(f32[5,8,18,1]{3,2,1,0:T(8,128)S(1)} %get-tuple-element.75), channel_id=1, source_target_pairs={{0,1},{1,2},{2,3},{3,4},{4,5},{5,6},{6,7},{8,9},{9,10},{10,11},{11... | collective-permute-start | bytes 8648 | tf_op jit(solution)/shard_map/ppermute | solution.py:18
  55.3 1.9 %collective-permute-start.3 = (f32[5,8,18,1]{3,2,1,0:T(8,128)S(1)}, f32[5,8,18,1]{3,2,1,0:T(8,128)S(1)}, u32[]{:S(2)}, u32[]{:S(2)}) collective-permute-start(f32[5,8,18,1]{3,2,1,0:T(8,128)S(1)} %get-tuple-element.76), channel_id=1, source_target_pairs={{1,0},{2,1},{3,2},{4,3},{5,4},{6,5},{7,6},{9,8},{10,9},{11,10},{12... | collective-permute-start | bytes 8648 | tf_op jit(solution)/shard_map/ppermute | solution.py:20
  57.2 3.8 %collective-permute-done.2 = f32[5,8,18,1]{3,2,1,0:T(8,128)S(1)} collective-permute-done((f32[5,8,18,1]{3,2,1,0:T(8,128)S(1)}, f32[5,8,18,1]{3,2,1,0:T(8,128)S(1)}, u32[]{:S(2)}, u32[]{:S(2)}) %collective-permute-start.2) | collective-permute-done | bytes 2912 | tf_op jit(solution)/shard_map/ppermute | solution.py:18
  61.0 4.4 %collective-permute-done.3 = f32[5,8,18,1]{3,2,1,0:T(8,128)S(1)} collective-permute-done((f32[5,8,18,1]{3,2,1,0:T(8,128)S(1)}, f32[5,8,18,1]{3,2,1,0:T(8,128)S(1)}, u32[]{:S(2)}, u32[]{:S(2)}) %collective-permute-start.3) | collective-permute-done | bytes 2912 | tf_op jit(solution)/shard_map/ppermute | solution.py:20
  66.2 1.0 fusion.142
  72.2 1.1 fusion.257
  73.9 1.0 fusion.233
  75.0 5.0 %copy.35 = f32[128,2,12,256]{3,1,0,2:T(2,128)} copy(f32[128,2,12,256]{3,1,2,0:T(2,128)} %all-to-all-done) | data formatting | bytes 6291456 | tf_op jit(solution)/shard_map/all_to_all | solution.py:175
  80.0 5.2 %reshape.417 = f32[256,12,256]{2,0,1:T(8,128)} reshape(f32[128,2,12,256]{3,1,0,2:T(2,128)} %copy.35) | data formatting | bytes 6291456 | tf_op jit(solution)/shard_map/reshape | solution.py:177
  85.2 3.0 %fusion = f32[4,12,208]{2,0,1:T(4,128)S(1)} fusion(f32[256,12,256]{2,0,1:T(8,128)} %reshape.417, s32[256]{0:T(256)S(1)} %copy-done.45, s32[4]{0:T(128)S(1)} %iota_add_fusion), kind=kOutput, calls=%fused_computation.3 | convolution fusion | flops 30671872 | bytes 3186704 | tf_op jit(solution)/shard_map/gk,kpq->gpq/dot_general | solution.py:179
  89.8 5.1 %collective-permute-start.4 = (f32[4,3,8,1,128]{4,3,2,1,0:T(1,128)S(1)}, f32[4,3,8,1,128]{4,3,2,1,0:T(1,128)S(1)}, u32[]{:S(2)}, u32[]{:S(2)}) collective-permute-start(f32[4,3,8,1,128]{4,3,2,1,0:T(1,128)S(1)} %get-tuple-element.50), channel_id=1, source_target_pairs={{0,8},{8,16},{16,24},{24,32},{32,40},{40,48},{48,56},{56,64},{64,7... | collective-permute-start | bytes 147464 | tf_op jit(solution)/shard_map/ppermute | solution.py:18
  94.9 1.9 %collective-permute-start.5 = (f32[4,3,8,1,128]{4,3,2,1,0:T(1,128)S(1)}, f32[4,3,8,1,128]{4,3,2,1,0:T(1,128)S(1)}, u32[]{:S(2)}, u32[]{:S(2)}) collective-permute-start(f32[4,3,8,1,128]{4,3,2,1,0:T(1,128)S(1)} %get-tuple-element.51), channel_id=1, source_target_pairs={{8,0},{16,8},{24,16},{32,24},{40,32},{48,40},{56,48},{64,56},{72,6... | collective-permute-start | bytes 147464 | tf_op jit(solution)/shard_map/ppermute | solution.py:20
  97.6 4.3 %collective-permute-done.5 = f32[4,3,8,1,128]{4,3,2,1,0:T(1,128)S(1)} collective-permute-done((f32[4,3,8,1,128]{4,3,2,1,0:T(1,128)S(1)}, f32[4,3,8,1,128]{4,3,2,1,0:T(1,128)S(1)}, u32[]{:S(2)}, u32[]{:S(2)}) %collective-permute-start.5) | collective-permute-done | bytes 49184 | tf_op jit(solution)/shard_map/ppermute | solution.py:20
  103.1 1.3 copy.42
  104.4 3.5 %collective-permute-start.6 = (f32[4,3,8,18,1]{3,2,4,1,0:T(8,128)}, f32[4,3,8,18,1]{3,2,4,1,0:T(8,128)S(1)}, u32[]{:S(2)}, u32[]{:S(2)}) collective-permute-start(f32[4,3,8,18,1]{3,2,4,1,0:T(8,128)} %copy.42), channel_id=1, source_target_pairs={{0,1},{1,2},{2,3},{3,4},{4,5},{5,6},{6,7},{8,9},{9,10},{10,11},{11... | collective-permute-start | bytes 20744 | tf_op jit(solution)/shard_map/ppermute | solution.py:18
  108.6 2.1 %collective-permute-start.7 = (f32[4,3,8,18,1]{3,2,4,1,0:T(8,128)S(1)}, f32[4,3,8,18,1]{3,2,4,1,0:T(8,128)}, u32[]{:S(2)}, u32[]{:S(2)}) collective-permute-start(f32[4,3,8,18,1]{3,2,4,1,0:T(8,128)S(1)} %copy.43), channel_id=1, source_target_pairs={{1,0},{2,1},{3,2},{4,3},{5,4},{6,5},{7,6},{9,8},{10,9},{11,10},{12... | collective-permute-start | bytes 20744 | tf_op jit(solution)/shard_map/ppermute | solution.py:20
  110.7 2.9 %fusion.211 = (f32[1,8,16,128]{3,2,1,0:T(8,128)}, f32[8,16,128]{2,1,0:T(8,128)}, f32[8,16,128]{2,1,0:T(8,128)}) fusion(f32[10,16,128]{2,1,0:T(8,128)} %get-tuple-element.156, f32[10,16,128]{2,1,0:T(8,128)} %get-tuple-element.155, f32[10,16,128]{2,1,0:T(8,128)} %get-tuple-element.140, f32[10,16,128]{2,1,0:T(8,128)} %get-tuple-element.139, ...), kind=kLoop, calls=%fused_computation.351 | loop fusion | flops 540672 | bytes 1703936 | tf_op jit(solution)/shard_map/stack | solution.py:89
  114.2 1.5 copy.45
  115.7 2.5 %pad_maximum_fusion = f32[4,3,8,18,130]{4,3,2,1,0:T(8,128)S(1)} fusion(f32[4,3,8,18,1]{4,3,2,1,0:T(8,128)S(1)} %copy.45, f32[4,3,8,1,128]{4,3,2,1,0:T(1,128)} %copy-done.39, f32[1,3,8,16,128]{4,3,2,1,0:T(8,128)} %copy-done.6, f32[1,3,8,16,128]{4,3,2,1,0:T(8,128)S(1)} %get-tuple-element.119, f32[1,3,8,16,128]{4,3,2,1,0:T(8,128)} %copy-done.7, ...), kind=kLoop, calls=%fused_computation.5 | loop fusion | flops 1572480 | bytes 1797120 | tf_op jit(solution)/shard_map/concatenate | solution.py:16
  127.7 1.9 %collective-permute-start.8 = (f32[3,8,1,128]{3,2,1,0:T(1,128)S(1)}, f32[3,8,1,128]{3,2,1,0:T(1,128)S(1)}, u32[]{:S(2)}, u32[]{:S(2)}) collective-permute-start(f32[3,8,1,128]{3,2,1,0:T(1,128)S(1)} %get-tuple-element.105), channel_id=1, source_target_pairs={{0,8},{8,16},{16,24},{24,32},{32,40},{40,48},{48,56},{56,64},{64,7... | collective-permute-start | bytes 36872 | tf_op jit(solution)/shard_map/ppermute | solution.py:18
  129.6 3.4 %collective-permute-start.9 = (f32[3,8,1,128]{3,2,1,0:T(1,128)S(1)}, f32[3,8,1,128]{3,2,1,0:T(1,128)S(1)}, u32[]{:S(2)}, u32[]{:S(2)}) collective-permute-start(f32[3,8,1,128]{3,2,1,0:T(1,128)S(1)} %get-tuple-element.106), channel_id=1, source_target_pairs={{8,0},{16,8},{24,16},{32,24},{40,32},{48,40},{56,48},{64,56},{72,6... | collective-permute-start | bytes 36872 | tf_op jit(solution)/shard_map/ppermute | solution.py:20
  133.0 3.2 %collective-permute-done.9 = f32[3,8,1,128]{3,2,1,0:T(1,128)S(1)} collective-permute-done((f32[3,8,1,128]{3,2,1,0:T(1,128)S(1)}, f32[3,8,1,128]{3,2,1,0:T(1,128)S(1)}, u32[]{:S(2)}, u32[]{:S(2)}) %collective-permute-start.9) | collective-permute-done | bytes 12320 | tf_op jit(solution)/shard_map/ppermute | solution.py:20
  136.4 4.8 %collective-permute-start.10 = (f32[3,8,18,1]{3,2,1,0:T(8,128)S(1)}, f32[3,8,18,1]{3,2,1,0:T(8,128)S(1)}, u32[]{:S(2)}, u32[]{:S(2)}) collective-permute-start(f32[3,8,18,1]{3,2,1,0:T(8,128)S(1)} %get-tuple-element.81), channel_id=1, source_target_pairs={{0,1},{1,2},{2,3},{3,4},{4,5},{5,6},{6,7},{8,9},{9,10},{10,11},{11... | collective-permute-start | bytes 5192 | tf_op jit(solution)/shard_map/ppermute | solution.py:18
  141.2 1.9 %collective-permute-start.11 = (f32[3,8,18,1]{3,2,1,0:T(8,128)S(1)}, f32[3,8,18,1]{3,2,1,0:T(8,128)S(1)}, u32[]{:S(2)}, u32[]{:S(2)}) collective-permute-start(f32[3,8,18,1]{3,2,1,0:T(8,128)S(1)} %get-tuple-element.82), channel_id=1, source_target_pairs={{1,0},{2,1},{3,2},{4,3},{5,4},{6,5},{7,6},{9,8},{10,9},{11,10},{12... | collective-permute-start | bytes 5192 | tf_op jit(solution)/shard_map/ppermute | solution.py:20
  143.9 0.9 collective-permute-done.10
  144.8 4.4 %collective-permute-done.11 = f32[3,8,18,1]{3,2,1,0:T(8,128)S(1)} collective-permute-done((f32[3,8,18,1]{3,2,1,0:T(8,128)S(1)}, f32[3,8,18,1]{3,2,1,0:T(8,128)S(1)}, u32[]{:S(2)}, u32[]{:S(2)}) %collective-permute-start.11) | collective-permute-done | bytes 1760 | tf_op jit(solution)/shard_map/ppermute | solution.py:20
  (201 shorter events, 29.6 us)
Async XLA Ops:
  5.8 11.0 %copy-start.41 = (f32[2,8,16,128]{3,2,1,0:T(8,128)S(1)}, f32[2,8,16,128]{3,2,1,0:T(8,128)}, u32[]{:S(2)}) copy-start(f32[2,8,16,128]{3,2,1,0:T(8,128)} %param.12) | copy-start | bytes 393220
  5.8 11.0 %copy-start.20 = (f32[3,8,16,128]{3,2,1,0:T(8,128)S(1)}, f32[3,8,16,128]{3,2,1,0:T(8,128)}, u32[]{:S(2)}) copy-start(f32[3,8,16,128]{3,2,1,0:T(8,128)} %param.9) | copy-start | bytes 589828
  5.8 16.4 %copy-start.44 = (s32[1,1,4,3]{2,1,3,0:T(1,128)S(1)}, s32[1,1,4,3]{2,1,3,0:T(1,128)}, u32[]{:S(2)}) copy-start(s32[1,1,4,3]{2,1,3,0:T(1,128)} %param.16) | copy-start | bytes 148
  5.8 17.1 %copy-start.43 = (s32[1,1,2]{2,1,0:T(1,128)S(1)}, s32[1,1,2]{2,1,0:T(1,128)}, u32[]{:S(2)}) copy-start(s32[1,1,2]{2,1,0:T(1,128)} %param.15) | copy-start | bytes 28
  5.8 17.7 %copy-start.42 = (f32[8,16,128]{2,1,0:T(8,128)S(1)}, f32[8,16,128]{2,1,0:T(8,128)}, u32[]{:S(2)}) copy-start(f32[8,16,128]{2,1,0:T(8,128)} %param.11) | copy-start | bytes 196612
  5.8 69.2 %all-to-all-start = ((f32[128,2,12,256]{3,1,2,0:T(2,128)}), f32[128,2,12,256]{3,1,2,0:T(2,128)}, u32[]{:S(2)}, u32[]{:S(2)}) async-start(f32[128,2,12,256]{3,1,2,0:T(2,128)} %broadcast_multiply_fusion), calls=%async_computation | async-start | bytes 6291456 | tf_op jit(solution)/shard_map/all_to_all | solution.py:175
  16.9 34.3 %collective-permute-start = (f32[5,8,1,128]{3,2,1,0:T(1,128)S(1)}, f32[5,8,1,128]{3,2,1,0:T(1,128)S(1)}, u32[]{:S(2)}, u32[]{:S(2)}) collective-permute-start(f32[5,8,1,128]{3,2,1,0:T(1,128)S(1)} %get-tuple-element.79), channel_id=1, source_target_pairs={{0,8},{8,16},{16,24},{24,32},{32,40},{40,48},{48,56},{56,64},{64,7... | collective-permute-start | bytes 61448 | tf_op jit(solution)/shard_map/ppermute | solution.py:18
  20.1 31.1 %collective-permute-start.1 = (f32[5,8,1,128]{3,2,1,0:T(1,128)S(1)}, f32[5,8,1,128]{3,2,1,0:T(1,128)S(1)}, u32[]{:S(2)}, u32[]{:S(2)}) collective-permute-start(f32[5,8,1,128]{3,2,1,0:T(1,128)S(1)} %get-tuple-element.80), channel_id=1, source_target_pairs={{8,0},{16,8},{24,16},{32,24},{40,32},{48,40},{56,48},{64,56},{72,6... | collective-permute-start | bytes 61448 | tf_op jit(solution)/shard_map/ppermute | solution.py:20
  51.5 9.6 %collective-permute-start.2 = (f32[5,8,18,1]{3,2,1,0:T(8,128)S(1)}, f32[5,8,18,1]{3,2,1,0:T(8,128)S(1)}, u32[]{:S(2)}, u32[]{:S(2)}) collective-permute-start(f32[5,8,18,1]{3,2,1,0:T(8,128)S(1)} %get-tuple-element.75), channel_id=1, source_target_pairs={{0,1},{1,2},{2,3},{3,4},{4,5},{5,6},{6,7},{8,9},{9,10},{10,11},{11... | collective-permute-start | bytes 8648 | tf_op jit(solution)/shard_map/ppermute | solution.py:18
  55.3 10.1 %collective-permute-start.3 = (f32[5,8,18,1]{3,2,1,0:T(8,128)S(1)}, f32[5,8,18,1]{3,2,1,0:T(8,128)S(1)}, u32[]{:S(2)}, u32[]{:S(2)}) collective-permute-start(f32[5,8,18,1]{3,2,1,0:T(8,128)S(1)} %get-tuple-element.76), channel_id=1, source_target_pairs={{1,0},{2,1},{3,2},{4,3},{5,4},{6,5},{7,6},{9,8},{10,9},{11,10},{12... | collective-permute-start | bytes 8648 | tf_op jit(solution)/shard_map/ppermute | solution.py:20
  66.2 2.0 %copy-start.2 = (f32[10,18,130]{2,1,0:T(8,128)}, f32[10,18,130]{2,1,0:T(8,128)S(1)}, u32[]{:S(2)}) copy-start(f32[10,18,130]{2,1,0:T(8,128)S(1)} %get-tuple-element.37) | copy-start | bytes 280804
  66.2 2.0 %copy-start.10 = (f32[10,18,130]{2,1,0:T(8,128)}, f32[10,18,130]{2,1,0:T(8,128)S(1)}, u32[]{:S(2)}) copy-start(f32[10,18,130]{2,1,0:T(8,128)S(1)} %get-tuple-element.41) | copy-start | bytes 280804
  66.2 7.1 %copy-start = (f32[10,18,130]{2,1,0:T(8,128)}, f32[10,18,130]{2,1,0:T(8,128)S(1)}, u32[]{:S(2)}) copy-start(f32[10,18,130]{2,1,0:T(8,128)S(1)} %get-tuple-element.38) | copy-start | bytes 280804
  68.2 5.1 %copy-start.9 = (f32[10,18,130]{2,1,0:T(8,128)}, f32[10,18,130]{2,1,0:T(8,128)S(1)}, u32[]{:S(2)}) copy-start(f32[10,18,130]{2,1,0:T(8,128)S(1)} %multiply_add_fusion) | copy-start | bytes 280804
  80.0 5.3 %copy-start.45 = (s32[256]{0:T(256)S(1)}, s32[256]{0:T(256)}, u32[]{:S(2)}) copy-start(s32[256]{0:T(256)} %param.14) | copy-start | bytes 3076
  89.5 8.1 %copy-start.3 = (f32[2,3,4,2,16,128]{5,4,3,1,0,2:T(8,128)}, f32[2,3,4,2,16,128]{5,4,3,1,0,2:T(8,128)S(1)}, u32[]{:S(2)}) copy-start(f32[2,3,4,2,16,128]{5,4,3,1,0,2:T(8,128)S(1)} %convolution_bitcast_fusion) | copy-start | bytes 1179652
  89.7 12.2 %copy-start.6 = (f32[1,3,8,16,128]{4,3,2,1,0:T(8,128)}, f32[1,3,8,16,128]{4,3,2,1,0:T(8,128)S(1)}, u32[]{:S(2)}) copy-start(f32[1,3,8,16,128]{4,3,2,1,0:T(8,128)S(1)} %get-tuple-element.120) | copy-start | bytes 589828
  89.7 12.2 %copy-start.7 = (f32[1,3,8,16,128]{4,3,2,1,0:T(8,128)}, f32[1,3,8,16,128]{4,3,2,1,0:T(8,128)S(1)}, u32[]{:S(2)}) copy-start(f32[1,3,8,16,128]{4,3,2,1,0:T(8,128)S(1)} %get-tuple-element.159) | copy-start | bytes 589828
  89.7 12.2 %copy-start.8 = (f32[1,3,8,16,128]{4,3,2,1,0:T(8,128)}, f32[1,3,8,16,128]{4,3,2,1,0:T(8,128)S(1)}, u32[]{:S(2)}) copy-start(f32[1,3,8,16,128]{4,3,2,1,0:T(8,128)S(1)} %get-tuple-element.160) | copy-start | bytes 589828
  89.8 7.7 %collective-permute-start.4 = (f32[4,3,8,1,128]{4,3,2,1,0:T(1,128)S(1)}, f32[4,3,8,1,128]{4,3,2,1,0:T(1,128)S(1)}, u32[]{:S(2)}, u32[]{:S(2)}) collective-permute-start(f32[4,3,8,1,128]{4,3,2,1,0:T(1,128)S(1)} %get-tuple-element.50), channel_id=1, source_target_pairs={{0,8},{8,16},{16,24},{24,32},{32,40},{40,48},{48,56},{56,64},{64,7... | collective-permute-start | bytes 147464 | tf_op jit(solution)/shard_map/ppermute | solution.py:18
  94.9 6.9 %collective-permute-start.5 = (f32[4,3,8,1,128]{4,3,2,1,0:T(1,128)S(1)}, f32[4,3,8,1,128]{4,3,2,1,0:T(1,128)S(1)}, u32[]{:S(2)}, u32[]{:S(2)}) collective-permute-start(f32[4,3,8,1,128]{4,3,2,1,0:T(1,128)S(1)} %get-tuple-element.51), channel_id=1, source_target_pairs={{8,0},{16,8},{24,16},{32,24},{40,32},{48,40},{56,48},{64,56},{72,6... | collective-permute-start | bytes 147464 | tf_op jit(solution)/shard_map/ppermute | solution.py:20
  97.6 4.3 %copy-start.38 = (f32[4,3,8,1,128]{4,3,2,1,0:T(1,128)}, f32[4,3,8,1,128]{4,3,2,1,0:T(1,128)S(1)}, u32[]{:S(2)}) copy-start(f32[4,3,8,1,128]{4,3,2,1,0:T(1,128)S(1)} %collective-permute-done.4) | copy-start | bytes 147460
  104.4 9.1 %collective-permute-start.6 = (f32[4,3,8,18,1]{3,2,4,1,0:T(8,128)}, f32[4,3,8,18,1]{3,2,4,1,0:T(8,128)S(1)}, u32[]{:S(2)}, u32[]{:S(2)}) collective-permute-start(f32[4,3,8,18,1]{3,2,4,1,0:T(8,128)} %copy.42), channel_id=1, source_target_pairs={{0,1},{1,2},{2,3},{3,4},{4,5},{5,6},{6,7},{8,9},{9,10},{10,11},{11... | collective-permute-start | bytes 20744 | tf_op jit(solution)/shard_map/ppermute | solution.py:18
  108.6 5.7 %collective-permute-start.7 = (f32[4,3,8,18,1]{3,2,4,1,0:T(8,128)S(1)}, f32[4,3,8,18,1]{3,2,4,1,0:T(8,128)}, u32[]{:S(2)}, u32[]{:S(2)}) collective-permute-start(f32[4,3,8,18,1]{3,2,4,1,0:T(8,128)S(1)} %copy.43), channel_id=1, source_target_pairs={{1,0},{2,1},{3,2},{4,3},{5,4},{6,5},{7,6},{9,8},{10,9},{11,10},{12... | collective-permute-start | bytes 20744 | tf_op jit(solution)/shard_map/ppermute | solution.py:20
  124.2 1.3 copy-start.18
  124.2 1.3 copy-start.19
  127.0 16.1 %copy-start.4 = (f32[2,3,4,2,16,128]{5,4,3,1,0,2:T(8,128)S(1)}, f32[2,3,4,2,16,128]{5,4,3,1,0,2:T(8,128)}, u32[]{:S(2)}) copy-start(f32[2,3,4,2,16,128]{5,4,3,1,0,2:T(8,128)} %copy-done.3) | copy-start | bytes 1179652
  127.7 24.6 %copy-start.5 = (f32[3,8,16,128]{3,2,1,0:T(8,128)}, f32[3,8,16,128]{3,2,1,0:T(8,128)S(1)}, u32[]{:S(2)}) copy-start(f32[3,8,16,128]{3,2,1,0:T(8,128)S(1)} %fusion.116) | copy-start | bytes 589828
  127.7 5.3 %collective-permute-start.8 = (f32[3,8,1,128]{3,2,1,0:T(1,128)S(1)}, f32[3,8,1,128]{3,2,1,0:T(1,128)S(1)}, u32[]{:S(2)}, u32[]{:S(2)}) collective-permute-start(f32[3,8,1,128]{3,2,1,0:T(1,128)S(1)} %get-tuple-element.105), channel_id=1, source_target_pairs={{0,8},{8,16},{16,24},{24,32},{32,40},{40,48},{48,56},{56,64},{64,7... | collective-permute-start | bytes 36872 | tf_op jit(solution)/shard_map/ppermute | solution.py:18
  129.6 6.5 %collective-permute-start.9 = (f32[3,8,1,128]{3,2,1,0:T(1,128)S(1)}, f32[3,8,1,128]{3,2,1,0:T(1,128)S(1)}, u32[]{:S(2)}, u32[]{:S(2)}) collective-permute-start(f32[3,8,1,128]{3,2,1,0:T(1,128)S(1)} %get-tuple-element.106), channel_id=1, source_target_pairs={{8,0},{16,8},{24,16},{32,24},{40,32},{48,40},{56,48},{64,56},{72,6... | collective-permute-start | bytes 36872 | tf_op jit(solution)/shard_map/ppermute | solution.py:20
  136.4 8.4 %collective-permute-start.10 = (f32[3,8,18,1]{3,2,1,0:T(8,128)S(1)}, f32[3,8,18,1]{3,2,1,0:T(8,128)S(1)}, u32[]{:S(2)}, u32[]{:S(2)}) collective-permute-start(f32[3,8,18,1]{3,2,1,0:T(8,128)S(1)} %get-tuple-element.81), channel_id=1, source_target_pairs={{0,1},{1,2},{2,3},{3,4},{4,5},{5,6},{6,7},{8,9},{9,10},{10,11},{11... | collective-permute-start | bytes 5192 | tf_op jit(solution)/shard_map/ppermute | solution.py:18
  141.2 8.0 %collective-permute-start.11 = (f32[3,8,18,1]{3,2,1,0:T(8,128)S(1)}, f32[3,8,18,1]{3,2,1,0:T(8,128)S(1)}, u32[]{:S(2)}, u32[]{:S(2)}) collective-permute-start(f32[3,8,18,1]{3,2,1,0:T(8,128)S(1)} %get-tuple-element.82), channel_id=1, source_target_pairs={{1,0},{2,1},{3,2},{4,3},{5,4},{6,5},{7,6},{9,8},{10,9},{11,10},{12... | collective-permute-start | bytes 5192 | tf_op jit(solution)/shard_map/ppermute | solution.py:20
  (27 other events, 25.2 us)
where the time goes:
time: 154 us; the launch traced here: 153 us
  waiting for transfers between devices  46.8 us (30%)
  starting transfers between devices  46.7 us (30%)
  local copies, waits for them, and re-layouts  29.4 us (19%)
  other arithmetic  23.6 us (15%)
  matrix products  4.95 us (3%)
  between operations  1.7 us (1%)
    ppermute x6, waiting for transfers between devices, padded_2(): lax.ppermute(tail, axis, [(i, (i + 1) % count) for i in range(ends)])  30.5 us
    ppermute x6, starting transfers between devices, padded_2(): lax.ppermute(tail, axis, [(i, (i + 1) % count) for i in range(ends)])  22.3 us
    ppermute x6, waiting for transfers between devices, padded_2(): lax.ppermute(head, axis, [((i + 1) % count, i) for i in range(ends)])  16.3 us
    ppermute x6, starting transfers between devices, padded_2(): lax.ppermute(head, axis, [((i + 1) % count, i) for i in range(ends)])  13.3 us
    all_to_all x1, starting transfers between devices, local(): lax.all_to_all(outgoing, ('gx', 'gy'), split_axis=0, concat_axis=0, tiled...  11 us
    another operation x10, other arithmetic, operate(): return jnp.stack(components, axis=-4)  7.81 us
    unnamed x95, local copies, waits for them, and re-layouts  7.05 us
    reshape x1, local copies, waits for them, and re-layouts, local(): received = lax.all_to_all(outgoing, ('gx', 'gy'), split_axis=0, concat_ax...  5.25 us
  transfers between devices with their start and end apart: 13, of which 7 were waited for; matrix products, arithmetic and copies ran while one was open for 12% of the time, Pallas kernels for 0%

commit v1 on v0

v1 whole, which is shorter than its diff:
```python
import jax
import jax.numpy as jnp
from jax import lax
from jax.experimental import pallas as pl
from jax.experimental.pallas import tpu as pltpu
from jax.sharding import PartitionSpec as P

step_square = 0.05
time_weights = ((-0.0595, 0.7735, 0.3315, -0.0455), (-0.063756, 0.607068, 0.517132, -0.060444))
NX, NY = 16, 8
LEV, CE, CN = 8, 16, 128
SLABS, PITCH = LEV + 2, 32
COARSE_EAST, COARSE_NORTH = 8, 26
WIDE = 384
MESH = pl.DeviceIdType.MESH
HIGHEST = lax.Precision.HIGHEST
F32 = jnp.float32
START, FORCE_0, FORCE_1, MIDDLE = range(4)
FIELDS = (5, 6, 6, 3)


def iota(shape, dim):
    return lax.broadcasted_iota(jnp.int32, shape, dim)


def dot(a, b):
    return jnp.dot(a, b, precision=HIGHEST, preferred_element_type=F32)


def hat(cells, points):
    return jnp.maximum(25 - jnp.abs(4 * cells - 25 * points), 0).astype(F32) * (1.0 / 25.0)


def kernel(
    now_h, prev_h, dens_h, mod_h, coarse_h, route_s, ranges_s, offs_s,
    inc_h, mid_h, nxt_h,
    prev_v, dens_v, coarse_v, timed_v, turned_v, pay_v, r1, out2, r2, q_v,
    ku0, kum, kup, oi0, oim, oip, md0, mdm, mdp,
    coef, base, inc_v, nxt_v,
    srows, scols, rrows, rcols, rcorn,
    hsend, hrecv, send1, recv1, send2, recv2, local_sem,
):
    gx = lax.axis_index("gx")
    gy = lax.axis_index("gy")

    def x_at(d):
        return lax.rem(gx + (d + NX), NX)

    def y_at(d):
        return lax.rem(gy + (d + NY), NY)

    copies_in = [
        pltpu.make_async_copy(coarse_h, coarse_v, local_sem.at[0]),
        pltpu.make_async_copy(mod_h, ku0.at[0:2, 1:9, 8:24, :], local_sem.at[1]),
        pltpu.make_async_copy(now_h, ku0.at[2:5, 1:9, 8:24, :], local_sem.at[2]),
        pltpu.make_async_copy(prev_h, prev_v, local_sem.at[3]),
        pltpu.make_async_copy(dens_h, dens_v, local_sem.at[4]),
    ]
    for copy in copies_in:
        copy.start()

    barrier = pltpu.get_barrier_semaphore()
    for d in range(1, NX):
        pl.semaphore_signal(barrier, inc=1, device_id=(x_at(d), gy), device_id_type=MESH)
    for d in range(1, NY):
        pl.semaphore_signal(barrier, inc=1, device_id=(gx, y_at(d)), device_id_type=MESH)
    for a in (-1, 1):
        for b in (-1, 1):
            pl.semaphore_signal(barrier, inc=1, device_id=(x_at(a), y_at(b)), device_id_type=MESH)

    copies_in[0].wait()
    for k in range(2):
        for n in range(2):
            row = (k * 2 + n) * 6
            total = None
            for t in range(4):
                term = time_weights[n][t] * coarse_v[k, t * 6:t * 6 + 6, :]
                total = term if total is None else total + term
            timed_v[row:row + 6, :] = total
    timed = timed_v[...]
    for a in range(COARSE_EAST):
        shifted = timed if a == 0 else pltpu.roll(timed, 256 - COARSE_NORTH * a, 1)
        turned_v[a * 24:(a + 1) * 24, :] = shifted[:, :128]
    lane8 = iota((8, 128), 1)
    for k in range(2):
        for tile in range(3):
            joined = None
            for part in range(4):
                piece = turned_v[pl.ds(k * 12 + tile * 4 + part, 8, stride=24), :]
                if part:
                    piece = pltpu.roll(piece, part * 32, 1)
                here = (lane8 >= part * 32) & (lane8 < part * 32 + COARSE_NORTH)
                joined = jnp.where(here, piece, 0.0 if joined is None else joined)
            pay_v[k * 8:(k + 1) * 8, tile * 128:(tile + 1) * 128] = joined

    pl.semaphore_wait(barrier, NX - 1 + NY - 1 + 4)

    own1 = pl.ds(pl.multiple_of(gx * 16, 16), 16)
    stage1 = [
        pltpu.make_async_remote_copy(
            pay_v, r1.at[own1, :], send1.at[d], recv1.at[d],
            device_id=(x_at(d), gy), device_id_type=MESH,
        )
        for d in range(1, NX)
    ]
    for copy in stage1:
        copy.start()
    r1[own1, :] = pay_v[...]

    lane16 = iota((16, 128), 1)
    has_low_x = gx > 0
    has_high_x = gx < NX - 1
    has_low_y = gy > 0
    has_high_y = gy < NY - 1

    def halo_copies(phase):
        count = FIELDS[phase] * 8
        rows_high, rows_low = srows.at[phase, 0, :count], srows.at[phase, 1, :count]
        cols_high, cols_low = scols.at[phase, 0], scols.at[phase, 1]
        plan = [
            (1, 0, rows_high, rrows.at[phase, 0, :count]),
            (-1, 0, rows_low, rrows.at[phase, 1, :count]),
            (0, 1, cols_high, rcols.at[phase, 0]),
            (0, -1, cols_low, rcols.at[phase, 1]),
            (1, 1, scols.at[phase, 0, 8:16], rcorn.at[phase, 0]),
            (1, -1, scols.at[phase, 1, 8:16], rcorn.at[phase, 1]),
            (-1, 1, scols.at[phase, 0, 0:8], rcorn.at[phase, 2]),
            (-1, -1, scols.at[phase, 1, 0:8], rcorn.at[phase, 3]),
        ]
        return [
            pltpu.make_async_remote_copy(
                src, dst, hsend.at[phase, i], hrecv.at[phase, i],
                device_id=(x_at(a), y_at(b)), device_id_type=MESH,
            )
            for i, (a, b, src, dst) in enumerate(plan)
        ]

    halos = [halo_copies(phase) for phase in range(4)]

    def send_edges(phase, pad, first):
        fields = FIELDS[phase]
        flat = pad.reshape(pad.shape[0] * SLABS * PITCH, CN)
        for f in range(fields):
            start = ((first + f) * SLABS + 1) * PITCH + 8
            srows[phase, 0, f * 8:(f + 1) * 8, :] = flat[pl.ds(start + CE - 1, 8, stride=PITCH), :]
            srows[phase, 1, f * 8:(f + 1) * 8, :] = flat[pl.ds(start, 8, stride=PITCH), :]
        halos[phase][0].start()
        halos[phase][1].start()

        def pack(level, carry):
            high, low = carry
            for f in range(fields):
                cells = pad[first + f, level + 1, 8:24, :]
                place = f * 8 + level
                here = lane16 == place
                high = jnp.where(here, pltpu.roll(cells, place + 1, 1), high)
                low = jnp.where(here, pltpu.roll(cells, place, 1), low)
            return high, low

        zero = jnp.zeros((16, 128), F32)
        high, low = lax.fori_loop(0, LEV, pack, (zero, zero))
        scols[phase, 0] = high
        scols[phase, 1] = low
        for copy in halos[phase][2:]:
            copy.start()

    def take_edges(phase, pads, first):
        pad, pad_m, pad_p = pads
        fields = FIELDS[phase]
        for copy in halos[phase]:
            copy.wait_recv()
        flats = [p.reshape(p.shape[0] * SLABS * PITCH, CN) for p in pads]
        sub8 = iota((8, 128), 0)

        def corner(which, row, keep):
            line = jnp.where(keep, rcorn[phase, which, row:row + 1, :], 0.0)
            return jnp.broadcast_to(line, (8, 128))

        corners = (
            (corner(0, 7, has_low_x & has_low_y), corner(1, 7, has_low_x & has_high_y)),
            (corner(2, 0, has_high_x & has_low_y), corner(3, 0, has_high_x & has_high_y)),
        )
        for f in range(fields):
            for side, keep in ((0, has_low_x), (1, has_high_x)):
                start = ((first + f) * SLABS + 1) * PITCH + (7 if side == 0 else 24)
                rows = jnp.where(keep, rrows[phase, side, f * 8:(f + 1) * 8, :], 0.0)
                mine = lane8 == sub8 + f * 8
                left = jnp.sum(jnp.where(mine, corners[side][0], 0.0), axis=1, keepdims=True)
                right = jnp.sum(jnp.where(mine, corners[side][1], 0.0), axis=1, keepdims=True)
                where = pl.ds(start, 8, stride=PITCH)
                flats[0][where, :] = rows
                flats[1][where, :] = jnp.where(lane8 == 0, left, pltpu.roll(rows, 1, 1))
                flats[2][where, :] = jnp.where(lane8 == 127, right, pltpu.roll(rows, 127, 1))
        low = jnp.where(has_low_y, rcols[phase, 0], 0.0)
        high = jnp.where(has_high_y, rcols[phase, 1], 0.0)

        def unpack(level, carry):
            for f in range(fields):
                cells = pad[first + f, level + 1, 8:24, :]
                place = f * 8 + level
                left = pltpu.roll(low, lax.rem(128 - place, 128), 1)
                right = pltpu.roll(high, 127 - place, 1)
                pad_m[first + f, level + 1, 8:24, :] = jnp.where(
                    lane16 == 0, left, pltpu.roll(cells, 1, 1)
                )
                pad_p[first + f, level + 1, 8:24, :] = jnp.where(
                    lane16 == 127, right, pltpu.roll(cells, 127, 1)
                )
            return carry

        lax.fori_loop(0, LEV, unpack, 0)

    blank = jnp.zeros((PITCH, CN), F32)
    for pads, fields in (((ku0, kum, kup), 5), ((oi0, oim, oip), 12), ((md0, mdm, mdp), 3)):

        def clear(f, carry, pads=pads):
            for pad in pads:
                pad[f, 0] = blank
                pad[f, SLABS - 1] = blank
            return carry

        lax.fori_loop(0, fields, clear, 0)

    copies_in[1].wait()
    copies_in[2].wait()
    send_edges(START, ku0, 0)

    tile = gx * NY + gy
    lane256 = iota((1, 256), 1)
    group = lax.div(lane256, 8)
    route = jnp.zeros((1, 256), jnp.int32)
    for x in range(NX):
        for k in range(2):
            route = jnp.where(group == x * 2 + k, route_s[(x * NY + gy) * 2 + k], route)
    row256 = iota((256, 256), 0)
    col256 = iota((256, 256), 1)
    wanted = gx * 32 + lax.div(row256, 8)
    select = jnp.where(
        (wanted == route) & (lax.rem(row256, 8) == lax.rem(col256, 8)), 1.0, 0.0
    ).astype(F32)
    east_rows = []
    for g in range(4):
        cells = iota((16, 256), 0) + offs_s[0, 0, g, 1]
        cols = iota((16, 256), 1)
        weights = hat(cells, lax.rem(cols, 8))
        east_rows.append(jnp.where(lax.rem(lax.div(cols, 8), 4) == g, weights, 0.0))
    east = jnp.concatenate(east_rows, axis=0)
    for g in range(4):
        point = iota((128, 256), 0)
        cell = iota((128, 256), 1)
        north = hat(lax.rem(cell, 128) + offs_s[0, 0, g, 2], lax.rem(point, 32))
        depth = (offs_s[0, 0, g, 0] + lax.div(cell, 128)).astype(F32) * (4.0 / 25.0)
        upright = jnp.where(point < 32, 1.0 - depth, depth)
        keep = (point < 64) & (lax.rem(point, 32) < COARSE_NORTH)
        q_v[g] = jnp.where(keep, north * upright, 0.0)

    for copy in stage1:
        copy.wait_recv()
    out2[...] = dot(select, r1[...])
    stage2 = []
    own2 = pl.ds(pl.multiple_of(gy * 32, 32), 32)
    for d in range(1, NY):
        to = y_at(d)
        stage2.append(
            pltpu.make_async_remote_copy(
                out2.at[pl.ds(pl.multiple_of(to * 32, 32), 32), :], r2.at[own2, :],
                send2.at[d], recv2.at[d], device_id=(gx, to), device_id_type=MESH,
            )
        )
    for copy in stage2:
        copy.start()
    r2[own2, :] = out2[own2, :]

    take_edges(START, (ku0, kum, kup), 0)
    ku = {-1: kum, 0: ku0, 1: kup}
    steps = ((1, 0, 0), (0, 1, 0), (0, 0, 1))

    def moved(d, sign):
        return tuple(sign * s for s in steps[d])

    def prepare(level, carry):
        def get(f, shift):
            dl, de, dn = shift
            return ku[dn][f, level + 1 + dl, 8 + de:24 + de, :]

        mu = get(0, (0, 0, 0))
        stiff = get(1, (0, 0, 0)) + 2.0 * mu
        shear_sides = []
        stiff_sides = []
        for d in range(3):
            for s in range(2):
                shift = moved(d, 1 - 2 * s)
                mu_side = get(0, shift)
                a = 0.5 * (mu + mu_side)
                b = 0.5 * (stiff + (get(1, shift) + 2.0 * mu_side))
                coef[d * 2 + s, level] = a
                coef[6 + d * 2 + s, level] = b
                shear_sides.append(a)
                stiff_sides.append(b)
        for i in range(3):
            total = None
            for d in range(3):
                sides = stiff_sides if d == i else shear_sides
                part = sides[2 * d] + sides[2 * d + 1]
                total = part if total is None else total + part
            coef[12 + i, level] = total
        dens_v[level] = step_square / dens_v[level]
        return carry

    def elastic(level, pads, index):
        cache = {}

        def get(c, shift):
            key = (c, shift)
            if key not in cache:
                dl, de, dn = shift
                cache[key] = pads[dn][index(c), level + 1 + dl, 8 + de:24 + de, :]
            return cache[key]

        kcache = {}

        def modulus(f, shift):
            key = (f, shift)
            if key not in kcache:
                dl, de, dn = shift
                kcache[key] = ku[dn][f, level + 1 + dl, 8 + de:24 + de, :]
            return kcache[key]

        def both(i, si, j, sj):
            a, b = moved(i, si), moved(j, sj)
            return tuple(p + q for p, q in zip(a, b))

        results = []
        for i in range(3):
            total = -coef[12 + i, level] * get(i, (0, 0, 0))
            for d in range(3):
                for s in range(2):
                    at = (6 if d == i else 0) + d * 2 + s
                    total = total + coef[at, level] * get(i, moved(d, 1 - 2 * s))
            mixed = None
            for j in range(3):
                if j == i:
                    continue
                pp = get(j, both(i, 1, j, 1))
                pm = get(j, both(i, 1, j, -1))
                mp = get(j, both(i, -1, j, 1))
                mm = get(j, both(i, -1, j, -1))
                part = (
                    modulus(1, moved(i, 1)) * (pp - pm)
                    - modulus(1, moved(i, -1)) * (mp - mm)
                    + modulus(0, moved(j, 1)) * (pp - mp)
                    - modulus(0, moved(j, -1)) * (pm - mm)
                )
                mixed = part if mixed is None else mixed + part
            results.append(total + 0.25 * mixed)
        return results

    copies_in[4].wait()
    lax.fori_loop(0, LEV, prepare, 0)
    copies_in[3].wait()

    def first_base(level, carry):
        applied = elastic(level, ku, lambda c: 2 + c)
        scale = dens_v[level]
        for c in range(3):
            now = ku0[2 + c, level + 1, 8:24, :]
            base[c, level] = 2.0 * now - prev_v[c, level] + scale * applied[c]
        return carry

    lax.fori_loop(0, LEV, first_base, 0)

    for copy in stage2:
        copy.wait_recv()
    low_level = ranges_s[0, 0, 0]
    high_level = ranges_s[0, 0, 1]
    eastern = dot(east, r2[...])
    for g in range(4):
        pieces = []
        for t in range(3):
            piece = eastern[g * 16:(g + 1) * 16, t * 128:(t + 1) * 128]
            pieces += [piece, pltpu.roll(piece, 64, 1)]
        fine = dot(jnp.concatenate(pieces, axis=0), q_v[g])
        for j in range(2):
            level = 2 * g + j
            outer = (level < low_level).astype(F32)
            inner = ((level >= low_level) & (level < high_level)).astype(F32)
            for n in range(2):
                for c in range(3):
                    p = n * 3 + c
                    cells = fine[p * 16:(p + 1) * 16, j * 128:(j + 1) * 128]
                    inc_v[n, c, level] = cells
                    oi0[n * 6 + c, level + 1, 8:24, :] = outer * cells
                    oi0[n * 6 + 3 + c, level + 1, 8:24, :] = inner * cells
    send_edges(FORCE_0, oi0, 0)
    send_edges(FORCE_1, oi0, 6)
    inc_out = pltpu.make_async_copy(inc_v, inc_h, local_sem.at[5])
    inc_out.start()

    oi = {-1: oim, 0: oi0, 1: oip}
    md = {-1: mdm, 0: md0, 1: mdp}

    def force(level, n):
        inside = (level >= low_level) & (level < high_level)
        which = n * 6 + jnp.where(inside, 0, 3)
        sign = inside.astype(F32) - (level < low_level).astype(F32)
        return sign, elastic(level, oi, lambda c: which + c)

    take_edges(FORCE_0, (oi0, oim, oip), 0)

    def middle(level, carry):
        sign, applied = force(level, 0)
        scale = sign * dens_v[level]
        for c in range(3):
            md0[c, level + 1, 8:24, :] = base[c, level] + scale * applied[c]
        return carry

    lax.fori_loop(0, LEV, middle, 0)
    send_edges(MIDDLE, md0, 0)
    mid_out = pltpu.make_async_copy(md0.at[:, 1:9, 8:24, :], mid_h, local_sem.at[6])
    mid_out.start()

    take_edges(FORCE_1, (oi0, oim, oip), 6)

    def second_base(level, carry):
        sign, applied = force(level, 1)
        scale = sign * dens_v[level]
        for c in range(3):
            mid = md0[c, level + 1, 8:24, :]
            now = ku0[2 + c, level + 1, 8:24, :]
            base[c, level] = 2.0 * mid - now + scale * applied[c]
        return carry

    lax.fori_loop(0, LEV, second_base, 0)
    take_edges(MIDDLE, (md0, mdm, mdp), 0)

    def last(level, carry):
        applied = elastic(level, md, lambda c: c)
        scale = dens_v[level]
        for c in range(3):
            nxt_v[c, level] = base[c, level] + scale * applied[c]
        return carry

    lax.fori_loop(0, LEV, last, 0)
    nxt_out = pltpu.make_async_copy(nxt_v, nxt_h, local_sem.at[7])
    nxt_out.start()
    for copy in stage1 + stage2:
        copy.wait_send()
    for phase in range(4):
        for copy in halos[phase]:
            copy.wait_send()
    inc_out.wait()
    mid_out.wait()
    nxt_out.wait()


def local(disp_now, disp_prev, density, moduli, coarse, block_route, ranges, offsets):
    hbm = pl.BlockSpec(memory_space=pl.ANY)
    smem = pl.BlockSpec(memory_space=pltpu.SMEM)

    def vmem(*shape):
        return pltpu.VMEM(shape, F32)

    dma = pltpu.SemaphoreType.DMA
    return pl.pallas_call(
        kernel,
        out_shape=(
            jax.ShapeDtypeStruct((2, 3, LEV, CE, CN), F32),
            jax.ShapeDtypeStruct((3, LEV, CE, CN), F32),
            jax.ShapeDtypeStruct((3, LEV, CE, CN), F32),
        ),
        in_specs=[hbm] * 5 + [smem] * 3,
        out_specs=(hbm, hbm, hbm),
        scratch_shapes=[
            vmem(3, LEV, CE, CN), vmem(LEV, CE, CN), vmem(2, 24, 256), vmem(24, 256),
            vmem(192, 128), vmem(16, WIDE), vmem(256, WIDE), vmem(256, WIDE), vmem(256, WIDE),
            vmem(4, 128, 256),
            *[vmem(5, SLABS, PITCH, CN)] * 3,
            *[vmem(12, SLABS, PITCH, CN)] * 3,
            *[vmem(3, SLABS, PITCH, CN)] * 3,
            vmem(15, LEV, CE, CN), vmem(3, LEV, CE, CN), vmem(2, 3, LEV, CE, CN),
            vmem(3, LEV, CE, CN),
            vmem(4, 2, 48, 128), vmem(4, 2, 16, 128),
            vmem(4, 2, 48, 128), vmem(4, 2, 16, 128), vmem(4, 4, 8, 128),
            dma((4, 8)), dma((4, 8)), dma((NX,)), dma((NX,)), dma((NY,)), dma((NY,)), dma((8,)),
        ],
        compiler_params=pltpu.CompilerParams(
            collective_id=0, has_side_effects=True, vmem_limit_bytes=48 * 1024 * 1024
        ),
    )(disp_now, disp_prev, density, moduli, coarse, block_route, ranges, offsets)


def solution(mesh):
    return jax.shard_map(
        local,
        mesh=mesh,
        in_specs=(
            P(None, None, "gx", "gy"),
            P(None, None, "gx", "gy"),
            P(None, "gx", "gy"),
            P(None, None, "gx", "gy"),
            P(("gx", "gy"), None, None),
            P(),
            P("gx", "gy", None),
            P("gx", "gy", None, None),
        ),
        out_specs=(
            P(None, None, None, "gx", "gy"),
            P(None, None, "gx", "gy"),
            P(None, None, "gx", "gy"),
        ),
        check_vma=False,
    )
```

time: 154 us -> 48 us (0.31)
  the two profiles are of different devices: /device:TPU:27 before, /device:TPU:1 now
where the time goes in v1:
time: 48 us; the launch traced here: 47.7 us
  Pallas kernels  39.7 us (83%)
  local copies, waits for them, and re-layouts  7.28 us (15%)
  between operations  0.66 us (1%)
    pallas_call x1, Pallas kernels, local(): pl.pallas_call(kernel, out_shape=(jax.ShapeDtypeStruct((2, 3, LEV, CE, CN...  39.7 us
    unnamed x18, local copies, waits for them, and re-layouts  7.28 us

profile of v1, /device:TPU:1, one launch (start us, length us, event | category | flops | bytes accessed | tf_op | source)
XLA Modules:
  0.0 47.7 jit_solution(9970924374587510815)
XLA Ops:
  0.6 0.0 copy-start.6
  0.6 0.0 copy-start.5
  0.7 0.8 %copy.11.offs_s = s32[1,1,4,3]{3,2,1,0:T(4,128)S(1)} copy(s32[1,1,4,3]{2,1,3,0:T(1,128)} %param.15) | data formatting | bytes 96 | tf_op args[7]
  1.4 0.0 copy-done.6
  1.4 0.0 copy-done.5
  1.4 0.0 copy-start
  1.4 0.9 %copy-done = f32[3,8,16,128]{3,2,1,0:T(8,128)S(1)} copy-done((f32[3,8,16,128]{3,2,1,0:T(8,128)S(1)}, f32[3,8,16,128]{3,2,1,0:T(8,128)}, u32[]{:S(2)}) %copy-start) | copy-done | bytes 196632
  2.4 0.0 copy-start.1
  2.4 0.9 %copy-done.1 = f32[3,8,16,128]{3,2,1,0:T(8,128)S(1)} copy-done((f32[3,8,16,128]{3,2,1,0:T(8,128)S(1)}, f32[3,8,16,128]{3,2,1,0:T(8,128)}, u32[]{:S(2)}) %copy-start.1) | copy-done | bytes 196632
  3.3 0.0 copy-start.2
  3.3 0.9 %copy-done.2 = f32[2,8,16,128]{3,2,1,0:T(8,128)S(1)} copy-done((f32[2,8,16,128]{3,2,1,0:T(8,128)S(1)}, f32[2,8,16,128]{3,2,1,0:T(8,128)}, u32[]{:S(2)}) %copy-start.2) | copy-done | bytes 131096
  4.2 0.0 copy-start.3
  4.2 0.8 %copy-done.3 = f32[8,16,128]{2,1,0:T(8,128)S(1)} copy-done((f32[8,16,128]{2,1,0:T(8,128)S(1)}, f32[8,16,128]{2,1,0:T(8,128)}, u32[]{:S(2)}) %copy-start.3) | copy-done | bytes 65560
  5.0 0.0 copy-start.4
  5.0 0.8 %copy-done.4 = f32[2,24,256]{2,1,0:T(8,128)S(1)} copy-done((f32[2,24,256]{2,1,0:T(8,128)S(1)}, f32[2,24,256]{2,1,0:T(8,128)}, u32[]{:S(2)}) %copy-start.4) | copy-done | bytes 49176
  5.8 39.7 %shard_map.103 = (f32[2,3,8,16,128]{4,3,2,1,0:T(8,128)S(1)}, f32[3,8,16,128]{3,2,1,0:T(8,128)S(1)}, f32[3,8,16,128]{3,2,1,0:T(8,128)S(1)}) custom-call(f32[3,8,16,128]{3,2,1,0:T(8,128)S(1)} %copy-done, f32[3,8,16,128]{3,2,1,0:T(8,128)S(1)} %copy-done.1, f32[8,16,128]{2,1,0:T(8,128)S(1)} %copy-done.3, f32[2,8,16,128]{3,2,1,0:T(8,128)S(1)} %copy-done.2, ...), custom_call_target="tpu_custom_call" | custom-call | tf_op jit(solution)/shard_map/pallas_call | solution.py:464
  45.6 0.7 %copy.15 = f32[2,3,8,16,128]{4,3,2,1,0:T(8,128)} copy(f32[2,3,8,16,128]{4,3,2,1,0:T(8,128)S(1)} %get-tuple-element.6) | data formatting | bytes 786432
  46.3 0.7 %copy.16 = f32[3,8,16,128]{3,2,1,0:T(8,128)} copy(f32[3,8,16,128]{3,2,1,0:T(8,128)S(1)} %get-tuple-element.7) | data formatting | bytes 393216
  47.0 0.7 %copy.17 = f32[3,8,16,128]{3,2,1,0:T(8,128)} copy(f32[3,8,16,128]{3,2,1,0:T(8,128)S(1)} %get-tuple-element.8) | data formatting | bytes 393216
Async XLA Ops:
  0.6 0.8 %copy-start.6 = (s32[1,1,2]{2,1,0:T(1,128)S(1)}, s32[1,1,2]{2,1,0:T(1,128)}, u32[]{:S(2)}) copy-start(s32[1,1,2]{2,1,0:T(1,128)} %ranges_s.1) | copy-start | bytes 28
  0.6 0.8 %copy-start.5 = (s32[256]{0:T(256)S(1)}, s32[256]{0:T(256)}, u32[]{:S(2)}) copy-start(s32[256]{0:T(256)} %route_s.1) | copy-start | bytes 3076
  1.4 0.9 %copy-start = (f32[3,8,16,128]{3,2,1,0:T(8,128)S(1)}, f32[3,8,16,128]{3,2,1,0:T(8,128)}, u32[]{:S(2)}) copy-start(f32[3,8,16,128]{3,2,1,0:T(8,128)} %now_h.1) | copy-start | bytes 589828
  2.4 0.9 %copy-start.1 = (f32[3,8,16,128]{3,2,1,0:T(8,128)S(1)}, f32[3,8,16,128]{3,2,1,0:T(8,128)}, u32[]{:S(2)}) copy-start(f32[3,8,16,128]{3,2,1,0:T(8,128)} %prev_h.1) | copy-start | bytes 589828
  3.3 0.9 %copy-start.2 = (f32[2,8,16,128]{3,2,1,0:T(8,128)S(1)}, f32[2,8,16,128]{3,2,1,0:T(8,128)}, u32[]{:S(2)}) copy-start(f32[2,8,16,128]{3,2,1,0:T(8,128)} %mod_h.1) | copy-start | bytes 393220
  4.2 0.8 %copy-start.3 = (f32[8,16,128]{2,1,0:T(8,128)S(1)}, f32[8,16,128]{2,1,0:T(8,128)}, u32[]{:S(2)}) copy-start(f32[8,16,128]{2,1,0:T(8,128)} %dens_h.1) | copy-start | bytes 196612
  5.0 0.8 %copy-start.4 = (f32[2,24,256]{2,1,0:T(8,128)S(1)}, f32[2,24,256]{2,1,0:T(8,128)}, u32[]{:S(2)}) copy-start(f32[2,24,256]{2,1,0:T(8,128)} %coarse_h.1) | copy-start | bytes 147460

commit v2 on v1

v2 whole, which is shorter than its diff:
```python
import jax
import jax.numpy as jnp
from jax import lax
from jax.experimental import pallas as pl
from jax.experimental.pallas import tpu as pltpu
from jax.sharding import PartitionSpec as P

step_square = 0.05
time_weights = ((-0.0595, 0.7735, 0.3315, -0.0455), (-0.063756, 0.607068, 0.517132, -0.060444))
NX, NY = 16, 8
LEV, CE, CN = 8, 16, 128
SLABS, PITCH = LEV + 2, 32
COARSE_EAST, COARSE_NORTH = 8, 26
MESH = pl.DeviceIdType.MESH
HIGHEST = lax.Precision.HIGHEST
F32 = jnp.float32
START, FORCE_0, FORCE_1, MIDDLE = range(4)


def iota(shape, dim):
    return lax.broadcasted_iota(jnp.int32, shape, dim)


def dot(a, b):
    return jnp.dot(a, b, precision=HIGHEST, preferred_element_type=F32)


def split(x):
    high = x.astype(jnp.bfloat16)
    rest = x - high.astype(F32)
    middle = rest.astype(jnp.bfloat16)
    low = (rest - middle.astype(F32)).astype(jnp.bfloat16)
    return high, middle, low


def dot_exact(whole, x):
    parts = [jnp.dot(whole, part, preferred_element_type=F32) for part in split(x)]
    return (parts[2] + parts[1]) + parts[0]


def kernel(
    now_h, prev_h, dens_h, mod_h, coarse_h, route_h, ranges_h, offs_h,
    inc_v, mid_v, nxt_v,
    route_s, ranges_s, offs_s, prev_v, dens_v, coarse_v, timed_v, turned_v,
    pay_v, r1, out2, r2, pick_v, east_a, east_b, q_v,
    ku0, kum, kup, oi0, oim, oip, md0, mdm, mdp,
    coef, base, srows, scols, rrows, rcols, row_masks,
    hsend, hrecv, send1, recv1, send2, recv2, local_sem,
):
    gx = lax.axis_index("gx")
    gy = lax.axis_index("gy")

    def x_at(d):
        return lax.rem(gx + (d + NX), NX)

    def y_at(d):
        return lax.rem(gy + (d + NY), NY)

    has_x = {1: gx < NX - 1, -1: gx > 0, 0: None}
    has_y = {1: gy < NY - 1, -1: gy > 0, 0: None}

    def has(a, b):
        if a and b:
            return has_x[a] & has_y[b]
        return has_x[a] if a else has_y[b]

    copies_in = [
        pltpu.make_async_copy(coarse_h, coarse_v, local_sem.at[0]),
        pltpu.make_async_copy(mod_h, ku0.at[0:2, 1:9, 8:24, :], local_sem.at[1]),
        pltpu.make_async_copy(now_h, ku0.at[2:5, 1:9, 8:24, :], local_sem.at[2]),
        pltpu.make_async_copy(prev_h, prev_v, local_sem.at[3]),
        pltpu.make_async_copy(dens_h, dens_v, local_sem.at[4]),
        pltpu.make_async_copy(route_h, route_s, local_sem.at[5]),
        pltpu.make_async_copy(ranges_h, ranges_s, local_sem.at[6]),
        pltpu.make_async_copy(offs_h, offs_s, local_sem.at[7]),
    ]
    for at in (0, 5, 6, 7, 1, 2, 3, 4):
        copies_in[at].start()

    barrier = pltpu.get_barrier_semaphore()
    for d in range(1, NX):
        pl.semaphore_signal(barrier, inc=1, device_id=(x_at(d), gy), device_id_type=MESH)
    for d in range(1, NY):
        pl.semaphore_signal(barrier, inc=1, device_id=(gx, y_at(d)), device_id_type=MESH)
    for a in (-1, 1):
        for b in (-1, 1):

            @pl.when(has(a, b))
            def _(a=a, b=b):
                pl.semaphore_signal(
                    barrier, inc=1, device_id=(gx + a, gy + b), device_id_type=MESH
                )

    lane8 = iota((8, 128), 1)
    sub8 = iota((8, 128), 0)
    lane16 = iota((16, 128), 1)

    copies_in[0].wait()
    for n in range(2):
        for k in range(2):
            row = (n * 2 + k) * 6
            total = None
            for t in range(4):
                term = time_weights[n][t] * coarse_v[k, t * 6:t * 6 + 6, :]
                total = term if total is None else total + term
            timed_v[row:row + 6, :] = total
    timed = timed_v[...]
    for a in range(COARSE_EAST):
        shifted = timed if a == 0 else pltpu.roll(timed, 256 - COARSE_NORTH * a, 1)
        turned_v[a * 24:(a + 1) * 24, :] = shifted[:, :128]
    for n in range(2):
        places = [[(n * 2 + k) * 6 + p for p in range(4)] for k in range(2)]
        places.append([(n * 2 + k) * 6 + p for k in range(2) for p in (4, 5)])
        for at, rows in enumerate(places):
            joined = None
            for part, row in enumerate(rows):
                piece = turned_v[pl.ds(row, 8, stride=24), :]
                if part:
                    piece = pltpu.roll(piece, part * 32, 1)
                here = (lane8 >= part * 32) & (lane8 < part * 32 + COARSE_NORTH)
                joined = jnp.where(here, piece, 0.0 if joined is None else joined)
            pay_v[n, at * 8:(at + 1) * 8, :] = joined

    for copy in copies_in[5:]:
        copy.wait()
    low_level = ranges_s[0, 0, 0]
    high_level = ranges_s[0, 0, 1]
    lane256 = iota((1, 256), 1)
    group = lax.div(lane256, 8)
    route = jnp.zeros((1, 256), jnp.int32)
    for x in range(NX):
        for k in range(2):
            route = jnp.where(group == k * NX + x, route_s[(x * NY + gy) * 2 + k], route)
    row256 = iota((256, 256), 0)
    col256 = iota((256, 256), 1)
    wanted = gx * 32 + lax.div(row256, 8)
    pick_v[...] = jnp.where(
        (wanted == route) & (lax.rem(row256, 8) == lax.rem(col256, 8)), 1.0, 0.0
    ).astype(jnp.bfloat16)

    def hat25(cells, points):
        return jnp.maximum(25 - jnp.abs(4 * cells - 25 * points), 0).astype(F32)

    for g in range(4):
        for ref, count in ((east_a, 4), (east_b, 2)):
            shape = (16, count * 64)
            cells = iota(shape, 0) + offs_s[0, 1, 0, g]
            cols = iota(shape, 1)
            weights = hat25(cells, lax.rem(cols, 8))
            mine = lax.rem(lax.div(cols, 8), count) == (g if count == 4 else g // 2)
            ref[g * 16:(g + 1) * 16, :] = jnp.where(mine, weights, 0.0).astype(jnp.bfloat16)
        point = iota((128, 256), 0)
        cell = iota((128, 256), 1)
        north = hat25(lax.rem(cell, 128) + offs_s[0, 2, 0, g], lax.rem(point, 32)) * (1.0 / 625.0)
        depth = (offs_s[0, 0, 0, g] + lax.div(cell, 128)).astype(F32) * (4.0 / 25.0)
        upright = jnp.where(point < 32, 1.0 - depth, depth)
        keep = (point < 64) & (lax.rem(point, 32) < COARSE_NORTH)
        q_v[g] = jnp.where(keep, north * upright, 0.0)

    blank = jnp.zeros((PITCH, CN), F32)
    for pads, fields in (((ku0, kum, kup), 5), ((oi0, oim, oip), 12), ((md0, mdm, mdp), 3)):

        def clear(f, carry, pads=pads):
            for pad in pads:
                pad[f, 0] = blank
                pad[f, SLABS - 1] = blank
            return carry

        lax.fori_loop(0, fields, clear, 0)

    WAYS = ((1, 0), (-1, 0), (1, 1), (1, -1), (-1, 1), (-1, -1), (0, 1), (0, -1))

    def halo_copies(phase):
        rows = 48 if phase == START else 24
        plan = []
        for i, (a, b) in enumerate(WAYS):
            if a:
                src = srows.at[phase, 0 if a > 0 else 1, :rows]
                dst = rrows.at[phase, i, :rows]
            else:
                src = scols.at[phase, i - 6]
                dst = rcols.at[phase, i - 6]
            plan.append(
                pltpu.make_async_remote_copy(
                    src, dst, hsend.at[phase, i], hrecv.at[phase, i],
                    device_id=(gx + a, gy + b), device_id_type=MESH,
                )
            )
        return plan

    halos = [halo_copies(phase) for phase in range(4)]

    def halo_start(phase, which):
        for i in which:

            @pl.when(has(*WAYS[i]))
            def _(i=i):
                halos[phase][i].start()

    def halo_wait(phase):
        for i, (a, b) in enumerate(WAYS):

            @pl.when(has(-a, -b))
            def _(i=i):
                halos[phase][i].wait_recv()

    def pack_rows(phase, flat, first, slab, pitch, fields):
        for f in range(fields):
            start = first + f * slab * pitch
            srows[phase, 0, f * 8:(f + 1) * 8, :] = flat[pl.ds(start + CE - 1, 8, stride=pitch), :]
            srows[phase, 1, f * 8:(f + 1) * 8, :] = flat[pl.ds(start, 8, stride=pitch), :]

    def pack_cols(phase, cells_at, fields, high, low):
        def pack(level, carry):
            high, low = carry
            for f in range(fields):
                cells = cells_at(f, level)
                place = f * 8 + level
                here = lane16 == place
                high = jnp.where(here, pltpu.roll(cells, place + 1, 1), high)
                low = jnp.where(here, pltpu.roll(cells, place, 1), low)
            return high, low

        high, low = lax.fori_loop(0, LEV, pack, (high, low))
        scols[phase, 0] = high
        scols[phase, 1] = low

    def flat_of(pad):
        return pad.reshape(pad.shape[0] * SLABS * PITCH, CN)

    def padded_cells(pad, first):
        return lambda f, level: pad[first + f, level + 1, 8:24, :]

    SIDES = ((0, 2, 3, -1, 7), (1, 4, 5, 1, 24))

    def take_rows(phase, f, masks):
        out = []
        for side, (own, left, right, a, row) in enumerate(SIDES):
            here = slice(f * 8, (f + 1) * 8)
            middle = jnp.where(has(a, 0), rrows[phase, own, here, :], 0.0)
            minus = jnp.where(has(a, -1), rrows[phase, left, here, :], 0.0)
            plus = jnp.where(has(a, 1), rrows[phase, right, here, :], 0.0)
            for oi in range(masks):
                m, lo, hi = middle, minus, plus
                if masks > 1:
                    m = m * row_masks[own, oi]
                    lo = lo * row_masks[left, oi]
                    hi = hi * row_masks[right, oi]
                out.append((
                    side, oi, row, m,
                    pltpu.roll(jnp.where(lane8 == 127, lo, m), 1, 1),
                    pltpu.roll(jnp.where(lane8 == 0, hi, m), 127, 1),
                ))
        return out

    def store_rows(flats, index, row, values):
        where = pl.ds((index * SLABS + 1) * PITCH + row, 8, stride=PITCH)
        for flat, value in zip(flats, values):
            flat[where, :] = value

    def side_cols(phase):
        low = jnp.where(has(0, -1), rcols[phase, 0], 0.0)
        high = jnp.where(has(0, 1), rcols[phase, 1], 0.0)
        return low, high

    def turn(pads, first, fields):
        pad, pad_m, pad_p = pads

        def body(level, carry):
            for f in range(fields):
                cells = pad[first + f, level + 1, 8:24, :]
                pad_m[first + f, level + 1, 8:24, :] = pltpu.roll(cells, 1, 1)
                pad_p[first + f, level + 1, 8:24, :] = pltpu.roll(cells, 127, 1)
            return carry

        lax.fori_loop(0, LEV, body, 0)

    def take_edges(phase, pads, fields):
        _, pad_m, pad_p = pads
        flats = [flat_of(p) for p in pads]
        for f in range(fields):
            for _, _, row, m, lo, hi in take_rows(phase, f, 1):
                store_rows(flats, f, row, (m, lo, hi))
        low, high = side_cols(phase)

        def body(level, carry):
            for f in range(fields):
                place = f * 8 + level
                left = pltpu.roll(low, lax.rem(128 - place, 128), 1)
                right = pltpu.roll(high, 127 - place, 1)
                at_m = pad_m[f, level + 1, 8:24, :]
                at_p = pad_p[f, level + 1, 8:24, :]
                pad_m[f, level + 1, 8:24, :] = jnp.where(lane16 == 0, left, at_m)
                pad_p[f, level + 1, 8:24, :] = jnp.where(lane16 == 127, right, at_p)
            return carry

        lax.fori_loop(0, LEV, body, 0)

    copies_in[1].wait()
    copies_in[2].wait()
    range_rows = jnp.where(sub8 == 0, low_level, high_level).astype(F32)
    pack_rows(START, flat_of(ku0), PITCH + 8, SLABS, PITCH, 5)
    for side in range(2):
        srows[START, side, 40:48, :] = range_rows
    range_cols = jnp.where(lane16 == 40, low_level, high_level).astype(F32)
    pack_cols(START, padded_cells(ku0, 0), 5, range_cols, range_cols)
    turn((ku0, kum, kup), 0, 5)

    diagonal = (has_x[1].astype(jnp.int32) + has_x[-1].astype(jnp.int32)) * (
        has_y[1].astype(jnp.int32) + has_y[-1].astype(jnp.int32)
    )
    pl.semaphore_wait(barrier, NX - 1 + NY - 1 + diagonal)

    stage1 = [
        [
            pltpu.make_async_remote_copy(
                pay_v.at[n], r1.at[n, gx], send1.at[n, d], recv1.at[n, d],
                device_id=(x_at(d), gy), device_id_type=MESH,
            )
            for d in range(1, NX)
        ]
        for n in range(2)
    ]
    stage2 = [[], []]

    def line_start(n):
        for copy in stage1[n]:
            copy.start()
        r1[n, gx] = pay_v[n]

    def slots_start(n):
        for copy in stage1[n]:
            copy.wait_recv()
        held = r1[n]
        first = jnp.swapaxes(held[:, 0:16, :].reshape(NX, 2, 8, 128), 0, 1).reshape(256, 128)
        second = held[:, 16:24, :].reshape(128, 128)
        second = jnp.concatenate([second, pltpu.roll(second, 64, 1)], axis=0)
        found = dot_exact(pick_v[...], jnp.concatenate([first, second], axis=1))
        out2[n, :, 0:32, :] = found[:, :128].reshape(NY, 32, 128)
        folded = found[:, 128:].reshape(NY, 2, 2, 8, 128)
        even = folded[:, :, 0].reshape(128, 128)
        odd = pltpu.roll(folded[:, :, 1].reshape(128, 128), 64, 1)
        lanes = iota((128, 128), 1)
        out2[n, :, 32:48, :] = jnp.where(lanes < 64, even, odd).reshape(NY, 16, 128)
        for d in range(1, NY):
            to = y_at(d)
            stage2[n].append(
                pltpu.make_async_remote_copy(
                    out2.at[n, to], r2.at[n, gy], send2.at[n, d], recv2.at[n, d],
                    device_id=(gx, to), device_id_type=MESH,
                )
            )
        for copy in stage2[n]:
            copy.start()
        r2[n, gy] = out2[n, gy]

    line_start(0)
    line_start(1)
    halo_start(START, range(8))
    slots_start(0)
    slots_start(1)

    halo_wait(START)
    take_edges(START, (ku0, kum, kup), 5)
    level8 = sub8.astype(F32)
    for i in range(6):
        low = rrows[START, i, 40:41, :]
        high = rrows[START, i, 41:42, :]
        row_masks[i, 0] = jnp.where(level8 < low, 1.0, 0.0)
        row_masks[i, 1] = jnp.where((level8 >= low) & (level8 < high), 1.0, 0.0)
    ku = {-1: kum, 0: ku0, 1: kup}
    steps = ((1, 0, 0), (0, 1, 0), (0, 0, 1))

    def moved(d, sign):
        return tuple(sign * s for s in steps[d])

    def prepare(level, carry):
        def get(f, shift):
            dl, de, dn = shift
            return ku[dn][f, level + 1 + dl, 8 + de:24 + de, :]

        mu = get(0, (0, 0, 0))
        stiff = get(1, (0, 0, 0)) + 2.0 * mu
        shear_sides = []
        stiff_sides = []
        for d in range(3):
            for s in range(2):
                shift = moved(d, 1 - 2 * s)
                mu_side = get(0, shift)
                a = 0.5 * (mu + mu_side)
                b = 0.5 * (stiff + (get(1, shift) + 2.0 * mu_side))
                coef[d * 2 + s, level] = a
                coef[6 + d * 2 + s, level] = b
                shear_sides.append(a)
                stiff_sides.append(b)
        for i in range(3):
            total = None
            for d in range(3):
                sides = stiff_sides if d == i else shear_sides
                part = sides[2 * d] + sides[2 * d + 1]
                total = part if total is None else total + part
            coef[12 + i, level] = total
        dens_v[level] = step_square / dens_v[level]
        return carry

    def elastic(level, pads, index):
        cache = {}

        def get(c, shift):
            key = (c, shift)
            if key not in cache:
                dl, de, dn = shift
                cache[key] = pads[dn][index(c), level + 1 + dl, 8 + de:24 + de, :]
            return cache[key]

        kcache = {}

        def modulus(f, shift):
            key = (f, shift)
            if key not in kcache:
                dl, de, dn = shift
                kcache[key] = ku[dn][f, level + 1 + dl, 8 + de:24 + de, :]
            return kcache[key]

        def both(i, si, j, sj):
            a, b = moved(i, si), moved(j, sj)
            return tuple(p + q for p, q in zip(a, b))

        results = []
        for i in range(3):
            total = -coef[12 + i, level] * get(i, (0, 0, 0))
            for d in range(3):
                for s in range(2):
                    at = (6 if d == i else 0) + d * 2 + s
                    total = total + coef[at, level] * get(i, moved(d, 1 - 2 * s))
            mixed = None
            for j in range(3):
                if j == i:
                    continue
                pp = get(j, both(i, 1, j, 1))
                pm = get(j, both(i, 1, j, -1))
                mp = get(j, both(i, -1, j, 1))
                mm = get(j, both(i, -1, j, -1))
                part = (
                    modulus(1, moved(i, 1)) * (pp - pm)
                    - modulus(1, moved(i, -1)) * (mp - mm)
                    + modulus(0, moved(j, 1)) * (pp - mp)
                    - modulus(0, moved(j, -1)) * (pm - mm)
                )
                mixed = part if mixed is None else mixed + part
            results.append(total + 0.25 * mixed)
        return results

    copies_in[4].wait()
    lax.fori_loop(0, LEV, prepare, 0)
    copies_in[3].wait()

    def first_base(level, carry):
        applied = elastic(level, ku, lambda c: 2 + c)
        scale = dens_v[level]
        for c in range(3):
            now = ku0[2 + c, level + 1, 8:24, :]
            base[c, level] = 2.0 * now - prev_v[c, level] + scale * applied[c]
        return carry

    lax.fori_loop(0, LEV, first_base, 0)

    def incident(n):
        for copy in stage2[n]:
            copy.wait_recv()
        got = r2[n]
        eastern_a = dot_exact(east_a[...], got[:, 0:32, :].reshape(256, 128))
        eastern_b = dot_exact(east_b[...], got[:, 32:48, :].reshape(128, 128))
        for g in range(4):
            piece_a = eastern_a[g * 16:(g + 1) * 16]
            piece_b = eastern_b[g * 16:(g + 1) * 16]
            if g % 2:
                piece_b = pltpu.roll(piece_b, 64, 1)
            pieces = [piece_a, pltpu.roll(piece_a, 64, 1), piece_b]
            fine = dot(jnp.concatenate(pieces, axis=0), q_v[g])
            for j in range(2):
                for c in range(3):
                    inc_v[n, c, 2 * g + j] = fine[c * 16:(c + 1) * 16, j * 128:(j + 1) * 128]
        phase = FORCE_0 + n
        flat = inc_v.reshape(6 * LEV * CE, CN)
        pack_rows(phase, flat, n * 3 * LEV * CE, LEV, CE, 3)
        halo_start(phase, range(6))
        zero = jnp.zeros((16, 128), F32)
        pack_cols(phase, lambda f, level: inc_v[n, f, level], 3, zero, zero)
        halo_start(phase, (6, 7))

    def mask_inside(n):
        def body(level, carry):
            outer = (level < low_level).astype(F32)
            inner = ((level >= low_level) & (level < high_level)).astype(F32)
            for c in range(3):
                cells = inc_v[n, c, level]
                values = (cells, pltpu.roll(cells, 1, 1), pltpu.roll(cells, 127, 1))
                for pad, value in zip((oi0, oim, oip), values):
                    pad[n * 6 + c, level + 1, 8:24, :] = outer * value
                    pad[n * 6 + 3 + c, level + 1, 8:24, :] = inner * value
            return carry

        lax.fori_loop(0, LEV, body, 0)

    def take_masked(n):
        phase = FORCE_0 + n
        halo_wait(phase)
        flats = [flat_of(p) for p in (oi0, oim, oip)]
        for c in range(3):
            for _, oi, row, m, lo, hi in take_rows(phase, c, 2):
                store_rows(flats, n * 6 + oi * 3 + c, row, (m, lo, hi))
        low, high = side_cols(phase)
        bounds = []
        for side in range(2):
            got = rcols[START, side]
            bounds.append([
                jnp.broadcast_to(got[:, 40 + b:41 + b], (16, 128)) for b in range(2)
            ])

        def body(level, carry):
            here = level.astype(F32)
            outer = [here < bounds[side][0] for side in range(2)]
            inner = [(here >= bounds[side][0]) & (here < bounds[side][1]) for side in range(2)]
            for c in range(3):
                place = c * 8 + level
                left = pltpu.roll(low, lax.rem(128 - place, 128), 1)
                right = pltpu.roll(high, 127 - place, 1)
                for oi, masks in ((0, outer), (1, inner)):
                    at = n * 6 + oi * 3 + c
                    at_m = oim[at, level + 1, 8:24, :]
                    at_p = oip[at, level + 1, 8:24, :]
                    new_m = jnp.where(masks[0], left, 0.0)
                    new_p = jnp.where(masks[1], right, 0.0)
                    oim[at, level + 1, 8:24, :] = jnp.where(lane16 == 0, new_m, at_m)
                    oip[at, level + 1, 8:24, :] = jnp.where(lane16 == 127, new_p, at_p)
            return carry

        lax.fori_loop(0, LEV, body, 0)

    incident(0)
    mask_inside(0)
    incident(1)

    oi = {-1: oim, 0: oi0, 1: oip}
    md = {-1: mdm, 0: md0, 1: mdp}

    def force(level, n):
        inside = (level >= low_level) & (level < high_level)
        which = n * 6 + jnp.where(inside, 0, 3)
        sign = inside.astype(F32) - (level < low_level).astype(F32)
        return sign, elastic(level, oi, lambda c: which + c)

    take_masked(0)

    def middle(level, carry):
        sign, applied = force(level, 0)
        scale = sign * dens_v[level]
        for c in range(3):
            cells = base[c, level] + scale * applied[c]
            md0[c, level + 1, 8:24, :] = cells
            mid_v[c, level] = cells
        return carry

    lax.fori_loop(0, LEV, middle, 0)
    pack_rows(MIDDLE, flat_of(md0), PITCH + 8, SLABS, PITCH, 3)
    halo_start(MIDDLE, range(6))
    zero = jnp.zeros((16, 128), F32)
    pack_cols(MIDDLE, padded_cells(md0, 0), 3, zero, zero)
    halo_start(MIDDLE, (6, 7))
    mask_inside(1)
    turn((md0, mdm, mdp), 0, 3)
    take_masked(1)

    def second_base(level, carry):
        sign, applied = force(level, 1)
        scale = sign * dens_v[level]
        for c in range(3):
            mid = md0[c, level + 1, 8:24, :]
            now = ku0[2 + c, level + 1, 8:24, :]
            base[c, level] = 2.0 * mid - now + scale * applied[c]
        return carry

    lax.fori_loop(0, LEV, second_base, 0)
    halo_wait(MIDDLE)
    take_edges(MIDDLE, (md0, mdm, mdp), 3)

    def last(level, carry):
        applied = elastic(level, md, lambda c: c)
        scale = dens_v[level]
        for c in range(3):
            nxt_v[c, level] = base[c, level] + scale * applied[c]
        return carry

    lax.fori_loop(0, LEV, last, 0)
    for n in range(2):
        for copy in stage1[n] + stage2[n]:
            copy.wait_send()
    for phase in range(4):
        for i, (a, b) in enumerate(WAYS):

            @pl.when(has(a, b))
            def _(i=i, phase=phase):
                halos[phase][i].wait_send()


def hand_out(inc_v, mid_v, nxt_v, inc_h, mid_h, nxt_h, sems):
    copies = [
        pltpu.make_async_copy(src, dst, sems.at[i])
        for i, (src, dst) in enumerate(((inc_v, inc_h), (mid_v, mid_h), (nxt_v, nxt_h)))
    ]
    for copy in copies:
        copy.start()
    for copy in copies:
        copy.wait()


def local(disp_now, disp_prev, density, moduli, coarse, block_route, ranges, offsets):
    hbm = pl.BlockSpec(memory_space=pl.ANY)
    on_chip = pl.BlockSpec(memory_space=pltpu.VMEM)

    def vmem(*shape):
        return pltpu.VMEM(shape, F32)

    dma = pltpu.SemaphoreType.DMA
    outs = (
        jax.ShapeDtypeStruct((2, 3, LEV, CE, CN), F32),
        jax.ShapeDtypeStruct((3, LEV, CE, CN), F32),
        jax.ShapeDtypeStruct((3, LEV, CE, CN), F32),
    )
    args = (
        disp_now, disp_prev, density, moduli, coarse, block_route, ranges,
        offsets.transpose(0, 3, 1, 2),
    )
    results = pl.pallas_call(
        kernel,
        out_shape=outs,
        in_specs=[hbm] * 8,
        out_specs=(on_chip,) * 3,
        scratch_shapes=[
            pltpu.SMEM((256,), jnp.int32), pltpu.SMEM((1, 1, 2), jnp.int32),
            pltpu.SMEM((1, 3, 1, 4), jnp.int32),
            vmem(3, LEV, CE, CN), vmem(LEV, CE, CN), vmem(2, 24, 256), vmem(24, 256),
            vmem(192, 128), vmem(2, 24, 128), vmem(2, NX, 24, 128), vmem(2, NY, 48, 128),
            vmem(2, NY, 48, 128), pltpu.VMEM((256, 256), jnp.bfloat16),
            pltpu.VMEM((64, 256), jnp.bfloat16), pltpu.VMEM((64, 128), jnp.bfloat16),
            vmem(4, 128, 256),
            *[vmem(5, SLABS, PITCH, CN)] * 3,
            *[vmem(12, SLABS, PITCH, CN)] * 3,
            *[vmem(3, SLABS, PITCH, CN)] * 3,
            vmem(15, LEV, CE, CN), vmem(3, LEV, CE, CN),
            vmem(4, 2, 48, 128), vmem(4, 2, 16, 128),
            vmem(4, 6, 48, 128), vmem(4, 2, 16, 128), vmem(6, 2, 8, 128),
            dma((4, 8)), dma((4, 8)), dma((2, NX)), dma((2, NX)), dma((2, NY)), dma((2, NY)),
            dma((8,)),
        ],
        compiler_params=pltpu.CompilerParams(
            collective_id=0, has_side_effects=True, vmem_limit_bytes=48 * 1024 * 1024
        ),
    )(*[pltpu.with_memory_space_constraint(v, pltpu.HBM) for v in args])
    return pl.pallas_call(
        hand_out,
        out_shape=outs,
        in_specs=[on_chip] * 3,
        out_specs=(hbm, hbm, hbm),
        scratch_shapes=[dma((3,))],
        compiler_params=pltpu.CompilerParams(vmem_limit_bytes=4 * 1024 * 1024),
    )(*results)


def solution(mesh):
    return jax.shard_map(
        local,
        mesh=mesh,
        in_specs=(
            P(None, None, "gx", "gy"),
            P(None, None, "gx", "gy"),
            P(None, "gx", "gy"),
            P(None, None, "gx", "gy"),
            P(("gx", "gy"), None, None),
            P(),
            P("gx", "gy", None),
            P("gx", "gy", None, None),
        ),
        out_specs=(
            P(None, None, None, "gx", "gy"),
            P(None, None, "gx", "gy"),
            P(None, None, "gx", "gy"),
        ),
        check_vma=False,
    )
```

time: 48 us -> 32.5 us (0.68)
  Pallas kernels: 39.7 us -> 31.8 us
  local copies, waits for them, and re-layouts: 7.28 us -> 0 us
    pallas_call x1 -> x2, Pallas kernels: 39.7 us -> 31.8 us  [the longest x1 30.9 us: local(): pl.pallas_call(kernel, out_shape=outs, in_specs=[hbm] * 8, out_specs=(on_...]
    unnamed x18 -> x0, local copies, waits for them, and re-layouts: 7.28 us -> none
where the time goes in v2:
time: 32.5 us; the launch traced here: 32.4 us
  Pallas kernels  31.8 us (98%)
  between operations  0.64 us (2%)
    pallas_call x1, Pallas kernels, local(): pl.pallas_call(kernel, out_shape=outs, in_specs=[hbm] * 8, out_specs=(on_...  30.9 us
    pallas_call x1, Pallas kernels, local(): pl.pallas_call(hand_out, out_shape=outs, in_specs=[on_chip] * 3, out_spec...  0.9 us

profile of v2, /device:TPU:1, one launch (start us, length us, event | category | flops | bytes accessed | tf_op | source)
XLA Modules:
  0.0 32.4 jit_solution(16646076708422562221)
XLA Ops:
  0.6 30.9 %shard_map.103 = (f32[2,3,8,16,128]{4,3,2,1,0:T(8,128)S(1)}, f32[3,8,16,128]{3,2,1,0:T(8,128)S(1)}, f32[3,8,16,128]{3,2,1,0:T(8,128)S(1)}) custom-call(f32[3,8,16,128]{3,2,1,0:T(8,128)} %now_h.1, f32[3,8,16,128]{3,2,1,0:T(8,128)} %prev_h.1, f32[8,16,128]{2,1,0:T(8,128)} %dens_h.1, f32[2,8,16,128]{3,2,1,0:T(8,128)} %mod_h.1, f32[2,24,256]{2,1,0:T(8,128)} %coarse_h.1, ...), custom_call_target="tpu_custom_call" | custom-call | tf_op jit(solution)/shard_map/pallas_call | solution.py:635
  31.5 0.9 %shard_map.104 = (f32[2,3,8,16,128]{4,3,2,1,0:T(8,128)}, f32[3,8,16,128]{3,2,1,0:T(8,128)}, f32[3,8,16,128]{3,2,1,0:T(8,128)}) custom-call(f32[2,3,8,16,128]{4,3,2,1,0:T(8,128)S(1)} %get-tuple-element.6.inc_v, f32[3,8,16,128]{3,2,1,0:T(8,128)S(1)} %get-tuple-element.7.mid_v, f32[3,8,16,128]{3,2,1,0:T(8,128)S(1)} %get-tuple-element.8.nxt_v), custom_call_target="tpu_custom_call" | custom-call | tf_op jit(solution)/shard_map/pallas_call | solution.py:661

commit v3 on v2

--- a/solution.py
+++ b/solution.py
@@ -12,17 +12,14 @@
 SLABS, PITCH = LEV + 2, 32
 COARSE_EAST, COARSE_NORTH = 8, 26
 MESH = pl.DeviceIdType.MESH
-HIGHEST = lax.Precision.HIGHEST
+FAR_X = (10, 9, 11, 6, 14, 7, 5, 13, 15, 8, 2, 4, 12, 1, 3)
+FAR_Y = (4, 3, 5, 2, 6, 1, 7)
 F32 = jnp.float32
 START, FORCE_0, FORCE_1, MIDDLE = range(4)
 
 
 def iota(shape, dim):
     return lax.broadcasted_iota(jnp.int32, shape, dim)
-
-
-def dot(a, b):
-    return jnp.dot(a, b, precision=HIGHEST, preferred_element_type=F32)
 
 
 def split(x):
@@ -42,7 +39,7 @@
     now_h, prev_h, dens_h, mod_h, coarse_h, route_h, ranges_h, offs_h,
     inc_v, mid_v, nxt_v,
     route_s, ranges_s, offs_s, prev_v, dens_v, coarse_v, timed_v, turned_v,
-    pay_v, r1, out2, r2, pick_v, east_a, east_b, q_v,
+    found_s, pay_v, r1_0, r1_1, out2, r2, east_a, east_b, q_high, q_low,
     ku0, kum, kup, oi0, oim, oip, md0, mdm, mdp,
     coef, base, srows, scols, rrows, rcols, row_masks,
     hsend, hrecv, send1, recv1, send2, recv2, local_sem,
@@ -66,8 +63,8 @@
 
     copies_in = [
         pltpu.make_async_copy(coarse_h, coarse_v, local_sem.at[0]),
-        pltpu.make_async_copy(mod_h, ku0.at[0:2, 1:9, 8:24, :], local_sem.at[1]),
-        pltpu.make_async_copy(now_h, ku0.at[2:5, 1:9, 8:24, :], local_sem.at[2]),
+        pltpu.make_async_copy(mod_h, ku0.at[3:5, 1:9, 8:24, :], local_sem.at[1]),
+        pltpu.make_async_copy(now_h, ku0.at[0:3, 1:9, 8:24, :], local_sem.at[2]),
         pltpu.make_async_copy(prev_h, prev_v, local_sem.at[3]),
         pltpu.make_async_copy(dens_h, dens_v, local_sem.at[4]),
         pltpu.make_async_copy(route_h, route_s, local_sem.at[5]),
@@ -119,44 +116,12 @@
                     piece = pltpu.roll(piece, part * 32, 1)
                 here = (lane8 >= part * 32) & (lane8 < part * 32 + COARSE_NORTH)
                 joined = jnp.where(here, piece, 0.0 if joined is None else joined)
-            pay_v[n, at * 8:(at + 1) * 8, :] = joined
+            pay_v[n, at] = joined
 
     for copy in copies_in[5:]:
         copy.wait()
     low_level = ranges_s[0, 0, 0]
     high_level = ranges_s[0, 0, 1]
-    lane256 = iota((1, 256), 1)
-    group = lax.div(lane256, 8)
-    route = jnp.zeros((1, 256), jnp.int32)
-    for x in range(NX):
-        for k in range(2):
-            route = jnp.where(group == k * NX + x, route_s[(x * NY + gy) * 2 + k], route)
-    row256 = iota((256, 256), 0)
-    col256 = iota((256, 256), 1)
-    wanted = gx * 32 + lax.div(row256, 8)
-    pick_v[...] = jnp.where(
-        (wanted == route) & (lax.rem(row256, 8) == lax.rem(col256, 8)), 1.0, 0.0
-    ).astype(jnp.bfloat16)
-
-    def hat25(cells, points):
-        return jnp.maximum(25 - jnp.abs(4 * cells - 25 * points), 0).astype(F32)
-
-    for g in range(4):
-        for ref, count in ((east_a, 4), (east_b, 2)):
-            shape = (16, count * 64)
-            cells = iota(shape, 0) + offs_s[0, 1, 0, g]
-            cols = iota(shape, 1)
-            weights = hat25(cells, lax.rem(cols, 8))
-            mine = lax.rem(lax.div(cols, 8), count) == (g if count == 4 else g // 2)
-            ref[g * 16:(g + 1) * 16, :] = jnp.where(mine, weights, 0.0).astype(jnp.bfloat16)
-        point = iota((128, 256), 0)
-        cell = iota((128, 256), 1)
-        north = hat25(lax.rem(cell, 128) + offs_s[0, 2, 0, g], lax.rem(point, 32)) * (1.0 / 625.0)
-        depth = (offs_s[0, 0, 0, g] + lax.div(cell, 128)).astype(F32) * (4.0 / 25.0)
-        upright = jnp.where(point < 32, 1.0 - depth, depth)
-        keep = (point < 64) & (lax.rem(point, 32) < COARSE_NORTH)
-        q_v[g] = jnp.where(keep, north * upright, 0.0)
-
     blank = jnp.zeros((PITCH, CN), F32)
     for pads, fields in (((ku0, kum, kup), 5), ((oi0, oim, oip), 12), ((md0, mdm, mdp), 3)):
 
@@ -168,12 +133,17 @@
 
         lax.fori_loop(0, fields, clear, 0)
 
-    WAYS = ((1, 0), (-1, 0), (1, 1), (1, -1), (-1, 1), (-1, -1), (0, 1), (0, -1))
+    WAYS = ((1, 1), (1, -1), (-1, 1), (-1, -1), (1, 0), (-1, 0), (0, 1), (0, -1))
+
+    def slot_of(f):
+        return f if f < 3 else f + 1
 
     def halo_copies(phase):
-        rows = 48 if phase == START else 24
         plan = []
         for i, (a, b) in enumerate(WAYS):
+            rows = 24
+            if phase == START:
+                rows = 32 if b else 48
             if a:
                 src = srows.at[phase, 0 if a > 0 else 1, :rows]
                 dst = rrows.at[phase, i, :rows]
@@ -204,24 +174,33 @@
             def _(i=i):
                 halos[phase][i].wait_recv()
 
+    def halo_sent(phase):
+        for i, (a, b) in enumerate(WAYS):
+
+            @pl.when(has(a, b))
+            def _(i=i):
+                halos[phase][i].wait_send()
+
     def pack_rows(phase, flat, first, slab, pitch, fields):
         for f in range(fields):
             start = first + f * slab * pitch
-            srows[phase, 0, f * 8:(f + 1) * 8, :] = flat[pl.ds(start + CE - 1, 8, stride=pitch), :]
-            srows[phase, 1, f * 8:(f + 1) * 8, :] = flat[pl.ds(start, 8, stride=pitch), :]
+            at = slot_of(f) * 8
+            srows[phase, 0, at:at + 8, :] = flat[pl.ds(start + CE - 1, 8, stride=pitch), :]
+            srows[phase, 1, at:at + 8, :] = flat[pl.ds(start, 8, stride=pitch), :]
 
     def pack_cols(phase, cells_at, fields, high, low):
         def pack(level, carry):
             high, low = carry
             for f in range(fields):
                 cells = cells_at(f, level)
-                place = f * 8 + level
+                place = slot_of(f) * 8 + level
                 here = lane16 == place
                 high = jnp.where(here, pltpu.roll(cells, place + 1, 1), high)
                 low = jnp.where(here, pltpu.roll(cells, place, 1), low)
             return high, low
 
-        high, low = lax.fori_loop(0, LEV, pack, (high, low))
+        for level in range(LEV):
+            high, low = pack(level, (high, low))
         scols[phase, 0] = high
         scols[phase, 1] = low
 
@@ -231,15 +210,17 @@
     def padded_cells(pad, first):
         return lambda f, level: pad[first + f, level + 1, 8:24, :]
 
-    SIDES = ((0, 2, 3, -1, 7), (1, 4, 5, 1, 24))
+    SIDES = ((4, 0, 1, -1, 7), (5, 2, 3, 1, 24))
 
     def take_rows(phase, f, masks):
         out = []
         for side, (own, left, right, a, row) in enumerate(SIDES):
-            here = slice(f * 8, (f + 1) * 8)
+            here = slice(slot_of(f) * 8, slot_of(f) * 8 + 8)
             middle = jnp.where(has(a, 0), rrows[phase, own, here, :], 0.0)
-            minus = jnp.where(has(a, -1), rrows[phase, left, here, :], 0.0)
-            plus = jnp.where(has(a, 1), rrows[phase, right, here, :], 0.0)
+            minus = plus = jnp.zeros((8, 128), F32)
+            if f < 3:
+                minus = jnp.where(has(a, -1), rrows[phase, left, here, :], 0.0)
+                plus = jnp.where(has(a, 1), rrows[phase, right, here, :], 0.0)
             for oi in range(masks):
                 m, lo, hi = middle, minus, plus
                 if masks > 1:
@@ -273,7 +254,8 @@
                 pad_p[first + f, level + 1, 8:24, :] = pltpu.roll(cells, 127, 1)
             return carry
 
-        lax.fori_loop(0, LEV, body, 0)
+        for level in range(LEV):
+            body(level, 0)
 
     def take_edges(phase, pads, fields):
         _, pad_m, pad_p = pads
@@ -285,8 +267,8 @@
 
         def body(level, carry):
             for f in range(fields):
-                place = f * 8 + level
-                left = pltpu.roll(low, lax.rem(128 - place, 128), 1)
+                place = slot_of(f) * 8 + level
+                left = pltpu.roll(low, (128 - place) % 128, 1)
                 right = pltpu.roll(high, 127 - place, 1)
                 at_m = pad_m[f, level + 1, 8:24, :]
                 at_p = pad_p[f, level + 1, 8:24, :]
@@ -294,15 +276,16 @@
                 pad_p[f, level + 1, 8:24, :] = jnp.where(lane16 == 127, right, at_p)
             return carry
 
-        lax.fori_loop(0, LEV, body, 0)
+        for level in range(LEV):
+            body(level, 0)
 
     copies_in[1].wait()
     copies_in[2].wait()
     range_rows = jnp.where(sub8 == 0, low_level, high_level).astype(F32)
     pack_rows(START, flat_of(ku0), PITCH + 8, SLABS, PITCH, 5)
     for side in range(2):
-        srows[START, side, 40:48, :] = range_rows
-    range_cols = jnp.where(lane16 == 40, low_level, high_level).astype(F32)
+        srows[START, side, 24:32, :] = range_rows
+    range_cols = jnp.where(lane16 == 24, low_level, high_level).astype(F32)
     pack_cols(START, padded_cells(ku0, 0), 5, range_cols, range_cols)
     turn((ku0, kum, kup), 0, 5)
 
@@ -311,13 +294,15 @@
     )
     pl.semaphore_wait(barrier, NX - 1 + NY - 1 + diagonal)
 
+    r1 = (r1_0, r1_1)
+
     stage1 = [
         [
             pltpu.make_async_remote_copy(
-                pay_v.at[n], r1.at[n, gx], send1.at[n, d], recv1.at[n, d],
+                pay_v.at[n], r1[n].at[pl.ds(gx * 3, 3)], send1.at[n, d], recv1.at[n, d],
                 device_id=(x_at(d), gy), device_id_type=MESH,
             )
-            for d in range(1, NX)
+            for d in FAR_X
         ]
         for n in range(2)
     ]
@@ -326,46 +311,88 @@
     def line_start(n):
         for copy in stage1[n]:
             copy.start()
-        r1[n, gx] = pay_v[n]
+        r1[n][pl.ds(gx * 3, 3)] = pay_v[n]
+
+    lane_half = lane8 < 64
 
     def slots_start(n):
         for copy in stage1[n]:
             copy.wait_recv()
-        held = r1[n]
-        first = jnp.swapaxes(held[:, 0:16, :].reshape(NX, 2, 8, 128), 0, 1).reshape(256, 128)
-        second = held[:, 16:24, :].reshape(128, 128)
-        second = jnp.concatenate([second, pltpu.roll(second, 64, 1)], axis=0)
-        found = dot_exact(pick_v[...], jnp.concatenate([first, second], axis=1))
-        out2[n, :, 0:32, :] = found[:, :128].reshape(NY, 32, 128)
-        folded = found[:, 128:].reshape(NY, 2, 2, 8, 128)
-        even = folded[:, :, 0].reshape(128, 128)
-        odd = pltpu.roll(folded[:, :, 1].reshape(128, 128), 64, 1)
-        lanes = iota((128, 128), 1)
-        out2[n, :, 32:48, :] = jnp.where(lanes < 64, even, odd).reshape(NY, 16, 128)
-        for d in range(1, NY):
+
+        def fill(to, carry):
+            halves = []
+            for g in range(4):
+                place = found_s[to * 4 + g]
+                at = jnp.clip(place - 1, 0, 3 * NX - 2)
+                k = lax.rem(at, 3)
+                first = r1[n][at]
+                second = r1[n][at - k + 2]
+                second = pltpu.roll(second, 64 * lax.rem(k + g, 2), 1)
+                out2[n, to, g * 8:(g + 1) * 8, :] = jnp.where(place > 0, first, 0.0)
+                halves.append(jnp.where(place > 0, second, 0.0))
+            for h in range(2):
+                joined = jnp.where(lane_half, halves[2 * h], halves[2 * h + 1])
+                out2[n, to, 32 + h * 8:40 + h * 8, :] = joined
+            return carry
+
+        for d in FAR_Y + (0,):
             to = y_at(d)
-            stage2[n].append(
-                pltpu.make_async_remote_copy(
-                    out2.at[n, to], r2.at[n, gy], send2.at[n, d], recv2.at[n, d],
-                    device_id=(gx, to), device_id_type=MESH,
-                )
+            fill(to, 0)
+            if d == 0:
+                continue
+            copy = pltpu.make_async_remote_copy(
+                out2.at[n, to], r2.at[n, gy], send2.at[n, d], recv2.at[n, d],
+                device_id=(gx, to), device_id_type=MESH,
             )
-        for copy in stage2[n]:
             copy.start()
+            stage2[n].append(copy)
         r2[n, gy] = out2[n, gy]
 
     line_start(0)
+    halo_start(START, range(8))
     line_start(1)
-    halo_start(START, range(8))
+
+    def find(slot, carry):
+        place = jnp.int32(0)
+        for x in range(NX):
+            for k in range(2):
+                named = route_s[(x * NY + gy) * 2 + k] == gx * 32 + slot
+                place = jnp.maximum(place, jnp.where(named, 1 + 3 * x + k, 0))
+        found_s[slot] = place
+        return carry
+
+    lax.fori_loop(0, NY * 4, find, 0)
+
+    def hat25(cells, points):
+        return jnp.maximum(25 - jnp.abs(4 * cells - 25 * points), 0).astype(F32)
+
+    for g in range(4):
+        for ref, count in ((east_a, 4), (east_b, 2)):
+            shape = (16, count * 8)
+            cells = iota(shape, 0) + offs_s[0, 1, 0, g]
+            cols = iota(shape, 1)
+            weights = hat25(cells, lax.rem(cols, 8))
+            mine = lax.div(cols, 8) == (g if count == 4 else g // 2)
+            ref[g * 16:(g + 1) * 16, :] = jnp.where(mine, weights, 0.0).astype(jnp.bfloat16)
+        point = iota((128, 256), 0)
+        cell = iota((128, 256), 1)
+        north = hat25(lax.rem(cell, 128) + offs_s[0, 2, 0, g], lax.rem(point, 32)) * (1.0 / 625.0)
+        depth = (offs_s[0, 0, 0, g] + lax.div(cell, 128)).astype(F32) * (4.0 / 25.0)
+        upright = jnp.where(point < 32, 1.0 - depth, depth)
+        keep = (point < 64) & (lax.rem(point, 32) < COARSE_NORTH)
+        weights = jnp.where(keep, north * upright, 0.0)
+        high = weights.astype(jnp.bfloat16)
+        q_high[g] = high
+        q_low[g] = (weights - high.astype(F32)).astype(jnp.bfloat16)
+
     slots_start(0)
-    slots_start(1)
 
     halo_wait(START)
     take_edges(START, (ku0, kum, kup), 5)
     level8 = sub8.astype(F32)
     for i in range(6):
-        low = rrows[START, i, 40:41, :]
-        high = rrows[START, i, 41:42, :]
+        low = rrows[START, i, 24:25, :]
+        high = rrows[START, i, 25:26, :]
         row_masks[i, 0] = jnp.where(level8 < low, 1.0, 0.0)
         row_masks[i, 1] = jnp.where((level8 >= low) & (level8 < high), 1.0, 0.0)
     ku = {-1: kum, 0: ku0, 1: kup}
@@ -379,16 +406,16 @@
             dl, de, dn = shift
             return ku[dn][f, level + 1 + dl, 8 + de:24 + de, :]
 
-        mu = get(0, (0, 0, 0))
-        stiff = get(1, (0, 0, 0)) + 2.0 * mu
+        mu = get(3, (0, 0, 0))
+        stiff = get(4, (0, 0, 0)) + 2.0 * mu
         shear_sides = []
         stiff_sides = []
         for d in range(3):
             for s in range(2):
                 shift = moved(d, 1 - 2 * s)
-                mu_side = get(0, shift)
+                mu_side = get(3, shift)
                 a = 0.5 * (mu + mu_side)
-                b = 0.5 * (stiff + (get(1, shift) + 2.0 * mu_side))
+                b = 0.5 * (stiff + (get(4, shift) + 2.0 * mu_side))
                 coef[d * 2 + s, level] = a
                 coef[6 + d * 2 + s, level] = b
                 shear_sides.append(a)
@@ -442,10 +469,10 @@
                 mp = get(j, both(i, -1, j, 1))
                 mm = get(j, both(i, -1, j, -1))
                 part = (
-                    modulus(1, moved(i, 1)) * (pp - pm)
-                    - modulus(1, moved(i, -1)) * (mp - mm)
-                    + modulus(0, moved(j, 1)) * (pp - mp)
-                    - modulus(0, moved(j, -1)) * (pm - mm)
+                    modulus(4, moved(i, 1)) * (pp - pm)
+                    - modulus(4, moved(i, -1)) * (mp - mm)
+                    + modulus(3, moved(j, 1)) * (pp - mp)
+                    - modulus(3, moved(j, -1)) * (pm - mm)
                 )
                 mixed = part if mixed is None else mixed + part
             results.append(total + 0.25 * mixed)
@@ -456,28 +483,37 @@
     copies_in[3].wait()
 
     def first_base(level, carry):
-        applied = elastic(level, ku, lambda c: 2 + c)
+        applied = elastic(level, ku, lambda c: c)
         scale = dens_v[level]
         for c in range(3):
-            now = ku0[2 + c, level + 1, 8:24, :]
+            now = ku0[c, level + 1, 8:24, :]
             base[c, level] = 2.0 * now - prev_v[c, level] + scale * applied[c]
         return carry
 
     lax.fori_loop(0, LEV, first_base, 0)
+
+    slots_start(1)
 
     def incident(n):
         for copy in stage2[n]:
             copy.wait_recv()
-        got = r2[n]
-        eastern_a = dot_exact(east_a[...], got[:, 0:32, :].reshape(256, 128))
-        eastern_b = dot_exact(east_b[...], got[:, 32:48, :].reshape(128, 128))
+        got = r2[n, 0]
+        for y in range(1, NY):
+            got = got + r2[n, y]
+        eastern_a = dot_exact(east_a[...], got[0:32])
+        eastern_b = dot_exact(east_b[...], got[32:48])
         for g in range(4):
             piece_a = eastern_a[g * 16:(g + 1) * 16]
             piece_b = eastern_b[g * 16:(g + 1) * 16]
             if g % 2:
                 piece_b = pltpu.roll(piece_b, 64, 1)
             pieces = [piece_a, pltpu.roll(piece_a, 64, 1), piece_b]
-            fine = dot(jnp.concatenate(pieces, axis=0), q_v[g])
+            high, middle, _ = split(jnp.concatenate(pieces, axis=0))
+            both = jnp.dot(
+                jnp.concatenate([high, middle], axis=0), q_high[g], preferred_element_type=F32
+            )
+            rest = jnp.dot(high, q_low[g], preferred_element_type=F32)
+            fine = both[:48] + (both[48:] + rest)
             for j in range(2):
                 for c in range(3):
                     inc_v[n, c, 2 * g + j] = fine[c * 16:(c + 1) * 16, j * 128:(j + 1) * 128]
@@ -491,8 +527,8 @@
 
     def mask_inside(n):
         def body(level, carry):
-            outer = (level < low_level).astype(F32)
-            inner = ((level >= low_level) & (level < high_level)).astype(F32)
+            outer = (low_level > level).astype(F32)
+            inner = ((low_level <= level) & (high_level > level)).astype(F32)
             for c in range(3):
                 cells = inc_v[n, c, level]
                 values = (cells, pltpu.roll(cells, 1, 1), pltpu.roll(cells, 127, 1))
@@ -501,7 +537,8 @@
                     pad[n * 6 + 3 + c, level + 1, 8:24, :] = inner * value
             return carry
 
-        lax.fori_loop(0, LEV, body, 0)
+        for level in range(LEV):
+            body(level, 0)
 
     def take_masked(n):
         phase = FORCE_0 + n
@@ -515,16 +552,16 @@
         for side in range(2):
             got = rcols[START, side]
             bounds.append([
-                jnp.broadcast_to(got[:, 40 + b:41 + b], (16, 128)) for b in range(2)
+                jnp.broadcast_to(got[:, 24 + b:25 + b], (16, 128)) for b in range(2)
             ])
 
         def body(level, carry):
-            here = level.astype(F32)
+            here = float(level)
             outer = [here < bounds[side][0] for side in range(2)]
             inner = [(here >= bounds[side][0]) & (here < bounds[side][1]) for side in range(2)]
             for c in range(3):
                 place = c * 8 + level
-                left = pltpu.roll(low, lax.rem(128 - place, 128), 1)
+                left = pltpu.roll(low, (128 - place) % 128, 1)
                 right = pltpu.roll(high, 127 - place, 1)
                 for oi, masks in ((0, outer), (1, inner)):
                     at = n * 6 + oi * 3 + c
@@ -536,7 +573,8 @@
                     oip[at, level + 1, 8:24, :] = jnp.where(lane16 == 127, new_p, at_p)
             return carry
 
-        lax.fori_loop(0, LEV, body, 0)
+        for level in range(LEV):
+            body(level, 0)
 
     incident(0)
     mask_inside(0)
@@ -577,11 +615,16 @@
         scale = sign * dens_v[level]
         for c in range(3):
             mid = md0[c, level + 1, 8:24, :]
-            now = ku0[2 + c, level + 1, 8:24, :]
+            now = ku0[c, level + 1, 8:24, :]
             base[c, level] = 2.0 * mid - now + scale * applied[c]
         return carry
 
     lax.fori_loop(0, LEV, second_base, 0)
+    for n in range(2):
+        for copy in stage1[n] + stage2[n]:
+            copy.wait_send()
+    for phase in (START, FORCE_0, FORCE_1):
+        halo_sent(phase)
     halo_wait(MIDDLE)
     take_edges(MIDDLE, (md0, mdm, mdp), 3)
 
@@ -593,15 +636,7 @@
         return carry
 
     lax.fori_loop(0, LEV, last, 0)
-    for n in range(2):
-        for copy in stage1[n] + stage2[n]:
-            copy.wait_send()
-    for phase in range(4):
-        for i, (a, b) in enumerate(WAYS):
-
-            @pl.when(has(a, b))
-            def _(i=i, phase=phase):
-                halos[phase][i].wait_send()
+    halo_sent(MIDDLE)
 
 
 def hand_out(inc_v, mid_v, nxt_v, inc_h, mid_h, nxt_h, sems):
@@ -641,10 +676,11 @@
             pltpu.SMEM((256,), jnp.int32), pltpu.SMEM((1, 1, 2), jnp.int32),
             pltpu.SMEM((1, 3, 1, 4), jnp.int32),
             vmem(3, LEV, CE, CN), vmem(LEV, CE, CN), vmem(2, 24, 256), vmem(24, 256),
-            vmem(192, 128), vmem(2, 24, 128), vmem(2, NX, 24, 128), vmem(2, NY, 48, 128),
-            vmem(2, NY, 48, 128), pltpu.VMEM((256, 256), jnp.bfloat16),
-            pltpu.VMEM((64, 256), jnp.bfloat16), pltpu.VMEM((64, 128), jnp.bfloat16),
-            vmem(4, 128, 256),
+            vmem(192, 128), pltpu.SMEM((NY * 4,), jnp.int32),
+            vmem(2, 3, 8, 128), vmem(NX * 3, 8, 128), vmem(NX * 3, 8, 128),
+            vmem(2, NY, 48, 128), vmem(2, NY, 48, 128),
+            pltpu.VMEM((64, 32), jnp.bfloat16), pltpu.VMEM((64, 16), jnp.bfloat16),
+            pltpu.VMEM((4, 128, 256), jnp.bfloat16), pltpu.VMEM((4, 128, 256), jnp.bfloat16),
             *[vmem(5, SLABS, PITCH, CN)] * 3,
             *[vmem(12, SLABS, PITCH, CN)] * 3,
             *[vmem(3, SLABS, PITCH, CN)] * 3,

time: 32.5 us -> 29.6 us (0.911); the launches traced: 32.4 us -> 29.1 us
  Pallas kernels: 31.8 us -> 28.5 us
    pallas_call x1, Pallas kernels: 30.9 us -> 27.6 us  [local(): pl.pallas_call(kernel, out_shape=outs, in_specs=[hbm] * 8, out_specs=(on_...]
where the time goes in v3:
time: 29.6 us; the launch traced here: 29.1 us
  Pallas kernels  28.5 us (96%)
  between operations  0.64 us (2%)
    pallas_call x1, Pallas kernels, local(): pl.pallas_call(kernel, out_shape=outs, in_specs=[hbm] * 8, out_specs=(on_...  27.6 us
    pallas_call x1, Pallas kernels, local(): pl.pallas_call(hand_out, out_shape=outs, in_specs=[on_chip] * 3, out_spec...  0.9 us

profile of v3, /device:TPU:1, one launch (start us, length us, event | category | flops | bytes accessed | tf_op | source)
XLA Modules:
  0.0 29.1 jit_solution(2722602255746536823)
XLA Ops:
  0.6 27.6 %shard_map.103 = (f32[2,3,8,16,128]{4,3,2,1,0:T(8,128)S(1)}, f32[3,8,16,128]{3,2,1,0:T(8,128)S(1)}, f32[3,8,16,128]{3,2,1,0:T(8,128)S(1)}) custom-call(f32[3,8,16,128]{3,2,1,0:T(8,128)} %now_h.1, f32[3,8,16,128]{3,2,1,0:T(8,128)} %prev_h.1, f32[8,16,128]{2,1,0:T(8,128)} %dens_h.1, f32[2,8,16,128]{3,2,1,0:T(8,128)} %mod_h.1, f32[2,24,256]{2,1,0:T(8,128)} %coarse_h.1, ...), custom_call_target="tpu_custom_call" | custom-call | tf_op jit(solution)/shard_map/pallas_call | solution.py:670
  28.2 0.9 %shard_map.104 = (f32[2,3,8,16,128]{4,3,2,1,0:T(8,128)}, f32[3,8,16,128]{3,2,1,0:T(8,128)}, f32[3,8,16,128]{3,2,1,0:T(8,128)}) custom-call(f32[2,3,8,16,128]{4,3,2,1,0:T(8,128)S(1)} %get-tuple-element.6.inc_v, f32[3,8,16,128]{3,2,1,0:T(8,128)S(1)} %get-tuple-element.7.mid_v, f32[3,8,16,128]{3,2,1,0:T(8,128)S(1)} %get-tuple-element.8.nxt_v), custom_call_target="tpu_custom_call" | custom-call | tf_op jit(solution)/shard_map/pallas_call | solution.py:697

commit v4 on v3

--- a/solution.py
+++ b/solution.py
@@ -71,7 +71,7 @@
         pltpu.make_async_copy(ranges_h, ranges_s, local_sem.at[6]),
         pltpu.make_async_copy(offs_h, offs_s, local_sem.at[7]),
     ]
-    for at in (0, 5, 6, 7, 1, 2, 3, 4):
+    for at in (0, 1, 2):
         copies_in[at].start()
 
     barrier = pltpu.get_barrier_semaphore()
@@ -87,6 +87,9 @@
                 pl.semaphore_signal(
                     barrier, inc=1, device_id=(gx + a, gy + b), device_id_type=MESH
                 )
+
+    for at in (5, 6, 7, 3, 4):
+        copies_in[at].start()
 
     lane8 = iota((8, 128), 1)
     sub8 = iota((8, 128), 0)
@@ -118,21 +121,6 @@
                 joined = jnp.where(here, piece, 0.0 if joined is None else joined)
             pay_v[n, at] = joined
 
-    for copy in copies_in[5:]:
-        copy.wait()
-    low_level = ranges_s[0, 0, 0]
-    high_level = ranges_s[0, 0, 1]
-    blank = jnp.zeros((PITCH, CN), F32)
-    for pads, fields in (((ku0, kum, kup), 5), ((oi0, oim, oip), 12), ((md0, mdm, mdp), 3)):
-
-        def clear(f, carry, pads=pads):
-            for pad in pads:
-                pad[f, 0] = blank
-                pad[f, SLABS - 1] = blank
-            return carry
-
-        lax.fori_loop(0, fields, clear, 0)
-
     WAYS = ((1, 1), (1, -1), (-1, 1), (-1, -1), (1, 0), (-1, 0), (0, 1), (0, -1))
 
     def slot_of(f):
@@ -152,7 +140,7 @@
                 dst = rcols.at[phase, i - 6]
             plan.append(
                 pltpu.make_async_remote_copy(
-                    src, dst, hsend.at[phase, i], hrecv.at[phase, i],
+                    src, dst, hsend.at[phase], hrecv.at[phase],
                     device_id=(gx + a, gy + b), device_id_type=MESH,
                 )
             )
@@ -167,19 +155,28 @@
             def _(i=i):
                 halos[phase][i].start()
 
+    count_x = has_x[1].astype(jnp.int32) + has_x[-1].astype(jnp.int32)
+    count_y = has_y[1].astype(jnp.int32) + has_y[-1].astype(jnp.int32)
+
+    def all_of(ref, sem):
+        return pltpu.make_async_copy(ref, ref, sem)
+
+    def halo_all(phase, sem):
+        side, corner = (48, 32) if phase == START else (24, 24)
+        flat = rrows.reshape(4 * 6 * 48, CN)
+        for nx in (1, 2):
+            for ny in (1, 2):
+                rows = nx * side + nx * ny * corner + ny * 16
+
+                @pl.when((count_x == nx) & (count_y == ny))
+                def _(rows=rows):
+                    all_of(flat.at[pl.ds(phase * 6 * 48, rows)], sem.at[phase]).wait()
+
     def halo_wait(phase):
-        for i, (a, b) in enumerate(WAYS):
-
-            @pl.when(has(-a, -b))
-            def _(i=i):
-                halos[phase][i].wait_recv()
+        halo_all(phase, hrecv)
 
     def halo_sent(phase):
-        for i, (a, b) in enumerate(WAYS):
-
-            @pl.when(has(a, b))
-            def _(i=i):
-                halos[phase][i].wait_send()
+        halo_all(phase, hsend)
 
     def pack_rows(phase, flat, first, slab, pitch, fields):
         for f in range(fields):
@@ -279,27 +276,14 @@
         for level in range(LEV):
             body(level, 0)
 
-    copies_in[1].wait()
-    copies_in[2].wait()
-    range_rows = jnp.where(sub8 == 0, low_level, high_level).astype(F32)
-    pack_rows(START, flat_of(ku0), PITCH + 8, SLABS, PITCH, 5)
-    for side in range(2):
-        srows[START, side, 24:32, :] = range_rows
-    range_cols = jnp.where(lane16 == 24, low_level, high_level).astype(F32)
-    pack_cols(START, padded_cells(ku0, 0), 5, range_cols, range_cols)
-    turn((ku0, kum, kup), 0, 5)
-
-    diagonal = (has_x[1].astype(jnp.int32) + has_x[-1].astype(jnp.int32)) * (
-        has_y[1].astype(jnp.int32) + has_y[-1].astype(jnp.int32)
-    )
-    pl.semaphore_wait(barrier, NX - 1 + NY - 1 + diagonal)
+    pl.semaphore_wait(barrier, NX - 1 + NY - 1 + count_x * count_y)
 
     r1 = (r1_0, r1_1)
 
     stage1 = [
         [
             pltpu.make_async_remote_copy(
-                pay_v.at[n], r1[n].at[pl.ds(gx * 3, 3)], send1.at[n, d], recv1.at[n, d],
+                pay_v.at[n], r1[n].at[pl.ds(gx * 3, 3)], send1.at[n], recv1.at[n],
                 device_id=(x_at(d), gy), device_id_type=MESH,
             )
             for d in FAR_X
@@ -316,8 +300,7 @@
     lane_half = lane8 < 64
 
     def slots_start(n):
-        for copy in stage1[n]:
-            copy.wait_recv()
+        all_of(r1[n].at[0:3 * (NX - 1)], recv1.at[n]).wait()
 
         def fill(to, carry):
             halves = []
@@ -341,7 +324,7 @@
             if d == 0:
                 continue
             copy = pltpu.make_async_remote_copy(
-                out2.at[n, to], r2.at[n, gy], send2.at[n, d], recv2.at[n, d],
+                out2.at[n, to], r2.at[n, gy], send2.at[n], recv2.at[n],
                 device_id=(gx, to), device_id_type=MESH,
             )
             copy.start()
@@ -349,8 +332,32 @@
         r2[n, gy] = out2[n, gy]
 
     line_start(0)
+    for copy in copies_in[5:]:
+        copy.wait()
+    low_level = ranges_s[0, 0, 0]
+    high_level = ranges_s[0, 0, 1]
+    copies_in[1].wait()
+    copies_in[2].wait()
+    range_rows = jnp.where(sub8 == 0, low_level, high_level).astype(F32)
+    pack_rows(START, flat_of(ku0), PITCH + 8, SLABS, PITCH, 5)
+    for side in range(2):
+        srows[START, side, 24:32, :] = range_rows
+    range_cols = jnp.where(lane16 == 24, low_level, high_level).astype(F32)
+    pack_cols(START, padded_cells(ku0, 0), 5, range_cols, range_cols)
+    turn((ku0, kum, kup), 0, 5)
+
     halo_start(START, range(8))
     line_start(1)
+    blank = jnp.zeros((PITCH, CN), F32)
+    for pads, fields in (((ku0, kum, kup), 5), ((oi0, oim, oip), 12), ((md0, mdm, mdp), 3)):
+
+        def clear(f, carry, pads=pads):
+            for pad in pads:
+                pad[f, 0] = blank
+                pad[f, SLABS - 1] = blank
+            return carry
+
+        lax.fori_loop(0, fields, clear, 0)
 
     def find(slot, carry):
         place = jnp.int32(0)
@@ -495,8 +502,7 @@
     slots_start(1)
 
     def incident(n):
-        for copy in stage2[n]:
-            copy.wait_recv()
+        all_of(r2.at[n, 0:NY - 1], recv2.at[n]).wait()
         got = r2[n, 0]
         for y in range(1, NY):
             got = got + r2[n, y]
@@ -621,8 +627,8 @@
 
     lax.fori_loop(0, LEV, second_base, 0)
     for n in range(2):
-        for copy in stage1[n] + stage2[n]:
-            copy.wait_send()
+        all_of(r1[n].at[0:3 * (NX - 1)], send1.at[n]).wait()
+        all_of(r2.at[n, 0:NY - 1], send2.at[n]).wait()
     for phase in (START, FORCE_0, FORCE_1):
         halo_sent(phase)
     halo_wait(MIDDLE)
@@ -687,7 +693,7 @@
             vmem(15, LEV, CE, CN), vmem(3, LEV, CE, CN),
             vmem(4, 2, 48, 128), vmem(4, 2, 16, 128),
             vmem(4, 6, 48, 128), vmem(4, 2, 16, 128), vmem(6, 2, 8, 128),
-            dma((4, 8)), dma((4, 8)), dma((2, NX)), dma((2, NX)), dma((2, NY)), dma((2, NY)),
+            dma((4,)), dma((4,)), dma((2,)), dma((2,)), dma((2,)), dma((2,)),
             dma((8,)),
         ],
         compiler_params=pltpu.CompilerParams(

time: 29.6 us -> 28.3 us (0.956)
  Pallas kernels: 28.5 us -> 27.1 us
    pallas_call x1, Pallas kernels: 27.6 us -> 26.2 us  [local(): pl.pallas_call(kernel, out_shape=outs, in_specs=[hbm] * 8, out_specs=(on_...]
where the time goes in v4:
time: 28.3 us; the launch traced here: 27.8 us
  Pallas kernels  27.1 us (96%)
  between operations  0.64 us (2%)
    pallas_call x1, Pallas kernels, local(): pl.pallas_call(kernel, out_shape=outs, in_specs=[hbm] * 8, out_specs=(on_...  26.2 us
    pallas_call x1, Pallas kernels, local(): pl.pallas_call(hand_out, out_shape=outs, in_specs=[on_chip] * 3, out_spec...  0.9 us

profile of v4, /device:TPU:1, one launch (start us, length us, event | category | flops | bytes accessed | tf_op | source)
XLA Modules:
  0.0 27.8 jit_solution(16682610664587837747)
XLA Ops:
  0.6 26.2 %shard_map.103 = (f32[2,3,8,16,128]{4,3,2,1,0:T(8,128)S(1)}, f32[3,8,16,128]{3,2,1,0:T(8,128)S(1)}, f32[3,8,16,128]{3,2,1,0:T(8,128)S(1)}) custom-call(f32[3,8,16,128]{3,2,1,0:T(8,128)} %now_h.1, f32[3,8,16,128]{3,2,1,0:T(8,128)} %prev_h.1, f32[8,16,128]{2,1,0:T(8,128)} %dens_h.1, f32[2,8,16,128]{3,2,1,0:T(8,128)} %mod_h.1, f32[2,24,256]{2,1,0:T(8,128)} %coarse_h.1, ...), custom_call_target="tpu_custom_call" | custom-call | tf_op jit(solution)/shard_map/pallas_call | solution.py:676
  26.9 0.9 %shard_map.104 = (f32[2,3,8,16,128]{4,3,2,1,0:T(8,128)}, f32[3,8,16,128]{3,2,1,0:T(8,128)}, f32[3,8,16,128]{3,2,1,0:T(8,128)}) custom-call(f32[2,3,8,16,128]{4,3,2,1,0:T(8,128)S(1)} %get-tuple-element.6.inc_v, f32[3,8,16,128]{3,2,1,0:T(8,128)S(1)} %get-tuple-element.7.mid_v, f32[3,8,16,128]{3,2,1,0:T(8,128)S(1)} %get-tuple-element.8.nxt_v), custom_call_target="tpu_custom_call" | custom-call | tf_op jit(solution)/shard_map/pallas_call | solution.py:703

commit v5 on v4

--- a/solution.py
+++ b/solution.py
@@ -12,6 +12,7 @@
 SLABS, PITCH = LEV + 2, 32
 COARSE_EAST, COARSE_NORTH = 8, 26
 MESH = pl.DeviceIdType.MESH
+PARTS = 4
 FAR_X = (10, 9, 11, 6, 14, 7, 5, 13, 15, 8, 2, 4, 12, 1, 3)
 FAR_Y = (4, 3, 5, 2, 6, 1, 7)
 F32 = jnp.float32
@@ -35,13 +36,68 @@
     return (parts[2] + parts[1]) + parts[0]
 
 
+steps = ((1, 0, 0), (0, 1, 0), (0, 0, 1))
+
+
+def moved(d, sign):
+    return tuple(sign * s for s in steps[d])
+
+
+def elastic_at(level, pads, index, ku, coef):
+    cache = {}
+
+    def get(c, shift):
+        key = (c, shift)
+        if key not in cache:
+            dl, de, dn = shift
+            cache[key] = pads[dn][index(c), level + 1 + dl, 8 + de:24 + de, :]
+        return cache[key]
+
+    kcache = {}
+
+    def modulus(f, shift):
+        key = (f, shift)
+        if key not in kcache:
+            dl, de, dn = shift
+            kcache[key] = ku[dn][f, level + 1 + dl, 8 + de:24 + de, :]
+        return kcache[key]
+
+    def both(i, si, j, sj):
+        a, b = moved(i, si), moved(j, sj)
+        return tuple(p + q for p, q in zip(a, b))
+
+    results = []
+    for i in range(3):
+        total = -coef[12 + i, level] * get(i, (0, 0, 0))
+        for d in range(3):
+            for s in range(2):
+                at = (6 if d == i else 0) + d * 2 + s
+                total = total + coef[at, level] * get(i, moved(d, 1 - 2 * s))
+        mixed = None
+        for j in range(3):
+            if j == i:
+                continue
+            pp = get(j, both(i, 1, j, 1))
+            pm = get(j, both(i, 1, j, -1))
+            mp = get(j, both(i, -1, j, 1))
+            mm = get(j, both(i, -1, j, -1))
+            part = (
+                modulus(4, moved(i, 1)) * (pp - pm)
+                - modulus(4, moved(i, -1)) * (mp - mm)
+                + modulus(3, moved(j, 1)) * (pp - mp)
+                - modulus(3, moved(j, -1)) * (pm - mm)
+            )
+            mixed = part if mixed is None else mixed + part
+        results.append(total + 0.25 * mixed)
+    return results
+
+
 def kernel(
     now_h, prev_h, dens_h, mod_h, coarse_h, route_h, ranges_h, offs_h,
-    inc_v, mid_v, nxt_v,
-    route_s, ranges_s, offs_s, prev_v, dens_v, coarse_v, timed_v, turned_v,
+    inc_v, mid_v, ku0, kum, kup, md0, mdm, mdp, coef, base, dens_v,
+    route_s, ranges_s, offs_s, prev_v, coarse_v, timed_v, turned_v,
     found_s, pay_v, r1_0, r1_1, out2, r2, east_a, east_b, q_high, q_low,
-    ku0, kum, kup, oi0, oim, oip, md0, mdm, mdp,
-    coef, base, srows, scols, rrows, rcols, row_masks,
+    oi0, oim, oip, srows, scols, rrows, rcols, row_masks,
     hsend, hrecv, send1, recv1, send2, recv2, local_sem,
 ):
     gx = lax.axis_index("gx")
@@ -146,17 +202,24 @@
             )
         return plan
 
-    halos = [halo_copies(phase) for phase in range(4)]
-
-    def halo_start(phase, which):
-        for i in which:
-
-            @pl.when(has(*WAYS[i]))
-            def _(i=i):
-                halos[phase][i].start()
-
     count_x = has_x[1].astype(jnp.int32) + has_x[-1].astype(jnp.int32)
     count_y = has_y[1].astype(jnp.int32) + has_y[-1].astype(jnp.int32)
+
+    halos = [halo_copies(phase) for phase in range(4)]
+
+    def halo_start(phase, which):
+        @pl.when(count_x + count_y == 4)
+        def _():
+            for i in which:
+                halos[phase][i].start()
+
+        @pl.when(count_x + count_y < 4)
+        def _():
+            for i in which:
+
+                @pl.when(has(*WAYS[i]))
+                def _(i=i):
+                    halos[phase][i].start()
 
     def all_of(ref, sem):
         return pltpu.make_async_copy(ref, ref, sem)
@@ -305,12 +368,11 @@
         def fill(to, carry):
             halves = []
             for g in range(4):
-                place = found_s[to * 4 + g]
-                at = jnp.clip(place - 1, 0, 3 * NX - 2)
-                k = lax.rem(at, 3)
-                first = r1[n][at]
-                second = r1[n][at - k + 2]
-                second = pltpu.roll(second, 64 * lax.rem(k + g, 2), 1)
+                slot = to * 4 + g
+                place = found_s[0, slot]
+                first = r1[n][jnp.clip(found_s[1, slot], 0, 3 * NX - 1)]
+                second = r1[n][jnp.clip(found_s[2, slot], 0, 3 * NX - 1)]
+                second = pltpu.roll(second, found_s[3, slot], 1)
                 out2[n, to, g * 8:(g + 1) * 8, :] = jnp.where(place > 0, first, 0.0)
                 halves.append(jnp.where(place > 0, second, 0.0))
             for h in range(2):
@@ -365,7 +427,12 @@
             for k in range(2):
                 named = route_s[(x * NY + gy) * 2 + k] == gx * 32 + slot
                 place = jnp.maximum(place, jnp.where(named, 1 + 3 * x + k, 0))
-        found_s[slot] = place
+        at = jnp.maximum(place - 1, 0)
+        k = lax.rem(at, 3)
+        found_s[0, slot] = place
+        found_s[1, slot] = at
+        found_s[2, slot] = at - k + 2
+        found_s[3, slot] = 64 * lax.rem(k + slot, 2)
         return carry
 
     lax.fori_loop(0, NY * 4, find, 0)
@@ -403,10 +470,6 @@
         row_masks[i, 0] = jnp.where(level8 < low, 1.0, 0.0)
         row_masks[i, 1] = jnp.where((level8 >= low) & (level8 < high), 1.0, 0.0)
     ku = {-1: kum, 0: ku0, 1: kup}
-    steps = ((1, 0, 0), (0, 1, 0), (0, 0, 1))
-
-    def moved(d, sign):
-        return tuple(sign * s for s in steps[d])
 
     def prepare(level, carry):
         def get(f, shift):
@@ -438,52 +501,7 @@
         return carry
 
     def elastic(level, pads, index):
-        cache = {}
-
-        def get(c, shift):
-            key = (c, shift)
-            if key not in cache:
-                dl, de, dn = shift
-                cache[key] = pads[dn][index(c), level + 1 + dl, 8 + de:24 + de, :]
-            return cache[key]
-
-        kcache = {}
-
-        def modulus(f, shift):
-            key = (f, shift)
-            if key not in kcache:
-                dl, de, dn = shift
-                kcache[key] = ku[dn][f, level + 1 + dl, 8 + de:24 + de, :]
-            return kcache[key]
-
-        def both(i, si, j, sj):
-            a, b = moved(i, si), moved(j, sj)
-            return tuple(p + q for p, q in zip(a, b))
-
-        results = []
-        for i in range(3):
-            total = -coef[12 + i, level] * get(i, (0, 0, 0))
-            for d in range(3):
-                for s in range(2):
-                    at = (6 if d == i else 0) + d * 2 + s
-                    total = total + coef[at, level] * get(i, moved(d, 1 - 2 * s))
-            mixed = None
-            for j in range(3):
-                if j == i:
-                    continue
-                pp = get(j, both(i, 1, j, 1))
-                pm = get(j, both(i, 1, j, -1))
-                mp = get(j, both(i, -1, j, 1))
-                mm = get(j, both(i, -1, j, -1))
-                part = (
-                    modulus(4, moved(i, 1)) * (pp - pm)
-                    - modulus(4, moved(i, -1)) * (mp - mm)
-                    + modulus(3, moved(j, 1)) * (pp - mp)
-                    - modulus(3, moved(j, -1)) * (pm - mm)
-                )
-                mixed = part if mixed is None else mixed + part
-            results.append(total + 0.25 * mixed)
-        return results
+        return elastic_at(level, pads, index, ku, coef)
 
     copies_in[4].wait()
     lax.fori_loop(0, LEV, prepare, 0)
@@ -606,7 +624,7 @@
             mid_v[c, level] = cells
         return carry
 
-    lax.fori_loop(0, LEV, middle, 0)
+    lax.fori_loop(0, LEV, middle, 0, unroll=2)
     pack_rows(MIDDLE, flat_of(md0), PITCH + 8, SLABS, PITCH, 3)
     halo_start(MIDDLE, range(6))
     zero = jnp.zeros((16, 128), F32)
@@ -634,24 +652,36 @@
     halo_wait(MIDDLE)
     take_edges(MIDDLE, (md0, mdm, mdp), 3)
 
+    halo_sent(MIDDLE)
+
+
+def finish(
+    inc_v, mid_v, ku0, kum, kup, md0, mdm, mdp, coef, base, dens_v,
+    inc_h, mid_h, nxt_h, nxt_v, sems,
+):
+    copies = [
+        pltpu.make_async_copy(inc_v, inc_h, sems.at[0]),
+        pltpu.make_async_copy(mid_v, mid_h, sems.at[1]),
+    ]
+    for copy in copies:
+        copy.start()
+    ku = {-1: kum, 0: ku0, 1: kup}
+    md = {-1: mdm, 0: md0, 1: mdp}
+
     def last(level, carry):
-        applied = elastic(level, md, lambda c: c)
+        applied = elastic_at(level, md, lambda c: c, ku, coef)
         scale = dens_v[level]
         for c in range(3):
             nxt_v[c, level] = base[c, level] + scale * applied[c]
         return carry
 
-    lax.fori_loop(0, LEV, last, 0)
-    halo_sent(MIDDLE)
-
-
-def hand_out(inc_v, mid_v, nxt_v, inc_h, mid_h, nxt_h, sems):
-    copies = [
-        pltpu.make_async_copy(src, dst, sems.at[i])
-        for i, (src, dst) in enumerate(((inc_v, inc_h), (mid_v, mid_h), (nxt_v, nxt_h)))
-    ]
-    for copy in copies:
+    for part in range(PARTS):
+        levels = LEV // PARTS
+        lax.fori_loop(part * levels, (part + 1) * levels, last, 0, unroll=2)
+        here = pl.ds(part * levels, levels)
+        copy = pltpu.make_async_copy(nxt_v.at[:, here], nxt_h.at[:, here], sems.at[2 + part])
         copy.start()
+        copies.append(copy)
     for copy in copies:
         copy.wait()
 
@@ -668,6 +698,15 @@
         jax.ShapeDtypeStruct((2, 3, LEV, CE, CN), F32),
         jax.ShapeDtypeStruct((3, LEV, CE, CN), F32),
         jax.ShapeDtypeStruct((3, LEV, CE, CN), F32),
+    )
+    def array(*shape):
+        return jax.ShapeDtypeStruct(shape, F32)
+
+    held = (
+        *outs[:2],
+        *[array(5, SLABS, PITCH, CN)] * 3,
+        *[array(3, SLABS, PITCH, CN)] * 3,
+        array(15, LEV, CE, CN), array(3, LEV, CE, CN), array(LEV, CE, CN),
     )
     args = (
         disp_now, disp_prev, density, moduli, coarse, block_route, ranges,
@@ -675,37 +714,34 @@
     )
     results = pl.pallas_call(
         kernel,
-        out_shape=outs,
+        out_shape=held,
         in_specs=[hbm] * 8,
-        out_specs=(on_chip,) * 3,
+        out_specs=(on_chip,) * len(held),
         scratch_shapes=[
             pltpu.SMEM((256,), jnp.int32), pltpu.SMEM((1, 1, 2), jnp.int32),
             pltpu.SMEM((1, 3, 1, 4), jnp.int32),
-            vmem(3, LEV, CE, CN), vmem(LEV, CE, CN), vmem(2, 24, 256), vmem(24, 256),
-            vmem(192, 128), pltpu.SMEM((NY * 4,), jnp.int32),
+            vmem(3, LEV, CE, CN), vmem(2, 24, 256), vmem(24, 256),
+            vmem(192, 128), pltpu.SMEM((4, NY * 4), jnp.int32),
             vmem(2, 3, 8, 128), vmem(NX * 3, 8, 128), vmem(NX * 3, 8, 128),
             vmem(2, NY, 48, 128), vmem(2, NY, 48, 128),
             pltpu.VMEM((64, 32), jnp.bfloat16), pltpu.VMEM((64, 16), jnp.bfloat16),
             pltpu.VMEM((4, 128, 256), jnp.bfloat16), pltpu.VMEM((4, 128, 256), jnp.bfloat16),
-            *[vmem(5, SLABS, PITCH, CN)] * 3,
             *[vmem(12, SLABS, PITCH, CN)] * 3,
-            *[vmem(3, SLABS, PITCH, CN)] * 3,
-            vmem(15, LEV, CE, CN), vmem(3, LEV, CE, CN),
             vmem(4, 2, 48, 128), vmem(4, 2, 16, 128),
             vmem(4, 6, 48, 128), vmem(4, 2, 16, 128), vmem(6, 2, 8, 128),
             dma((4,)), dma((4,)), dma((2,)), dma((2,)), dma((2,)), dma((2,)),
             dma((8,)),
         ],
         compiler_params=pltpu.CompilerParams(
-            collective_id=0, has_side_effects=True, vmem_limit_bytes=48 * 1024 * 1024
+            collective_id=0, has_side_effects=True, vmem_limit_bytes=40 * 1024 * 1024
         ),
     )(*[pltpu.with_memory_space_constraint(v, pltpu.HBM) for v in args])
     return pl.pallas_call(
-        hand_out,
+        finish,
         out_shape=outs,
-        in_specs=[on_chip] * 3,
+        in_specs=[on_chip] * len(held),
         out_specs=(hbm, hbm, hbm),
-        scratch_shapes=[dma((3,))],
+        scratch_shapes=[vmem(3, LEV, CE, CN), dma((2 + PARTS,))],
         compiler_params=pltpu.CompilerParams(vmem_limit_bytes=4 * 1024 * 1024),
     )(*results)
 

time: 28.3 us -> 27.9 us (0.986)
  Pallas kernels: 27.1 us -> 26.7 us
    pallas_call x2, Pallas kernels: 27.1 us -> 26.7 us  [the longest x1 25.7 us: local(): pl.pallas_call(kernel, out_shape=held, in_specs=[hbm] * 8, out_specs=(on_...]
where the time goes in v5:
time: 27.9 us; the launch traced here: 27.4 us
  Pallas kernels  26.7 us (96%)
  between operations  0.64 us (2%)
    pallas_call x1, Pallas kernels, local(): pl.pallas_call(kernel, out_shape=held, in_specs=[hbm] * 8, out_specs=(on_...  25.7 us
    pallas_call x1, Pallas kernels, local(): pl.pallas_call(finish, out_shape=outs, in_specs=[on_chip] * len(held), ou...  1.01 us

profile of v5, /device:TPU:1, one launch (start us, length us, event | category | flops | bytes accessed | tf_op | source)
XLA Modules:
  0.0 27.4 jit_solution(5063102431817833767)
XLA Ops:
  0.6 25.7 %shard_map.103 = (f32[2,3,8,16,128]{4,3,2,1,0:T(8,128)S(1)}, f32[3,8,16,128]{3,2,1,0:T(8,128)S(1)}, f32[5,10,32,128]{3,2,1,0:T(8,128)S(1)}, f32[5,10,32,128]{3,2...) custom-call(f32[3,8,16,128]{3,2,1,0:T(8,128)} %now_h.1, ...), custom_call_target="tpu_custom_call" | custom-call | tf_op jit(solution)/shard_map/pallas_call | solution.py:715
  26.4 1.0 %shard_map.104 = (f32[2,3,8,16,128]{4,3,2,1,0:T(8,128)}, f32[3,8,16,128]{3,2,1,0:T(8,128)}, f32[3,8,16,128]{3,2,1,0:T(8,128)}) custom-call(f32[2,3,8,16,128]{4,3,2,1,0:T(8,128)S(1)} %get-tuple-element.14.inc_v, f32[3,8,16,128]{3,2,1,0:T(8,128)S(1)} %get-tuple-element.15.mid_v, f32[5,10,32,128]{3,2,1,0:T(8,128)S(1)} %get-tuple-element.16.ku0, ...), custom_call_target="tpu_custom_call" | custom-call | tf_op jit(solution)/shard_map/pallas_call | solution.py:739

commit v6 on v5

--- a/solution.py
+++ b/solution.py
@@ -603,6 +603,7 @@
     incident(0)
     mask_inside(0)
     incident(1)
+    mask_inside(1)
 
     oi = {-1: oim, 0: oi0, 1: oip}
     md = {-1: mdm, 0: md0, 1: mdp}
@@ -630,7 +631,6 @@
     zero = jnp.zeros((16, 128), F32)
     pack_cols(MIDDLE, padded_cells(md0, 0), 3, zero, zero)
     halo_start(MIDDLE, (6, 7))
-    mask_inside(1)
     turn((md0, mdm, mdp), 0, 3)
     take_masked(1)
 

time: 27.9 us -> 27.9 us (level)
  no operation moved by 1% of the time
where the time goes in v6:
time: 27.9 us; the launch traced here: 27.4 us
  Pallas kernels  26.7 us (96%)
  between operations  0.64 us (2%)
    pallas_call x1, Pallas kernels, local(): pl.pallas_call(kernel, out_shape=held, in_specs=[hbm] * 8, out_specs=(on_...  25.7 us
    pallas_call x1, Pallas kernels, local(): pl.pallas_call(finish, out_shape=outs, in_specs=[on_chip] * len(held), ou...  1.01 us

profile of v6, /device:TPU:1, one launch (start us, length us, event | category | flops | bytes accessed | tf_op | source)
XLA Modules:
  0.0 27.4 jit_solution(1191006428154969439)
XLA Ops:
  0.6 25.7 %shard_map.103 = (f32[2,3,8,16,128]{4,3,2,1,0:T(8,128)S(1)}, f32[3,8,16,128]{3,2,1,0:T(8,128)S(1)}, f32[5,10,32,128]{3,2,1,0:T(8,128)S(1)}, f32[5,10,32,128]{3,2...) custom-call(f32[3,8,16,128]{3,2,1,0:T(8,128)} %now_h.1, ...), custom_call_target="tpu_custom_call" | custom-call | tf_op jit(solution)/shard_map/pallas_call | solution.py:715
  26.4 1.0 %shard_map.104 = (f32[2,3,8,16,128]{4,3,2,1,0:T(8,128)}, f32[3,8,16,128]{3,2,1,0:T(8,128)}, f32[3,8,16,128]{3,2,1,0:T(8,128)}) custom-call(f32[2,3,8,16,128]{4,3,2,1,0:T(8,128)S(1)} %get-tuple-element.14.inc_v, f32[3,8,16,128]{3,2,1,0:T(8,128)S(1)} %get-tuple-element.15.mid_v, f32[5,10,32,128]{3,2,1,0:T(8,128)S(1)} %get-tuple-element.16.ku0, ...), custom_call_target="tpu_custom_call" | custom-call | tf_op jit(solution)/shard_map/pallas_call | solution.py:739
